TPU v7x, 128 devices: a whole 4x4x4 slice. The times are simulated.
128 devices in a mesh: wave: 32 (over z, x_lo, y), lev: 4 (over x_hi, core).
Axes of the slice: x: 4 (x_hi: 2, x_lo: 2; x = x_hi * 2 + x_lo), y: 4, z: 4, core: 2. Of those that a mesh axis runs over, the one named last changes fastest.
Arguments:
- spectral: bfloat16 [2, 16, 640, 1281], P(None, 'lev', 'wave'), may hold values from -6 to 6
- legendre: bfloat16 [640, 1281, 256], P(('wave', 'lev')), may hold values from -0.0048828125 to 0.0048828125
- wave_table: int32 [640], replicated, may hold values from 0 to 639, each once
- courant_lon: float32 [16, 256, 5120], P('lev', 'wave'), may hold values from -0.35 to 0.35
- courant_lat: float32 [16, 256, 5120], P('lev', 'wave'), may hold values from -0.35 to 0.35
Outputs:
- tracer: float32 [16, 256, 5120], P('lev', 'wave')
Inputs may be any that keep to these rules, and one draw needn't show every extreme that they name: A permutation of the pairs: slot s carries wavenumbers wave_table[s] and 1279 - wave_table[s].
All inputs are finite; a program needn't handle non-finite values.
Results may differ from a plain program's by a relative error of at most 0.003.
Values may be sent and summed in bfloat16 or wider, within the bound.
A program may use at most 64 MiB of HBM per device.

v0:
```python
import math

import jax
import jax.numpy as jnp
from jax import lax
from jax.sharding import PartitionSpec as P

M = 1280
NLON = 5120
FA = 64
FB = 80
PASSES = 4


def padded(value, sides, width):
    for axis, dim in sides:
        devices, length = (lax.axis_size(axis), value.shape[dim])
        up = [(i, (i + 1) % devices) for i in range(devices - 1)]
        down = [(j, i) for i, j in up]
        last = lax.slice_in_dim(value, length - width, length, axis=dim)
        initial = lax.slice_in_dim(value, 0, width, axis=dim)
        before = lax.ppermute(last, axis, up)
        after = lax.ppermute(initial, axis, down)
        value = jnp.concatenate([before, value, after], axis=dim)
    return value


def donor_flux(left_side, right_side, speed):
    return jnp.maximum(speed, 0.0) * left_side + jnp.minimum(speed, 0.0) * right_side


def from_west(field):
    return jnp.roll(field, 1, axis=-1)


def from_east(field):
    return jnp.roll(field, -1, axis=-1)


def floored_ratio(numerator, denominator):
    return numerator / jnp.maximum(denominator, 1.0)


def mpdata_pass(tracer_rows, speed_lon, speed_lat, inside):
    flux_lon = donor_flux(from_west(tracer_rows), tracer_rows, speed_lon)
    flux_lat = donor_flux(tracer_rows[..., :-1, :], tracer_rows[..., 1:, :], speed_lat[..., 1:, :])
    upwind = (
        tracer_rows[..., 1:-1, :]
        - (from_east(flux_lon) - flux_lon)[..., 1:-1, :]
        - (flux_lat[..., 1:, :] - flux_lat[..., :-1, :])
    )
    upwind = jnp.where(inside[1:-1, None], upwind, 0.0)
    west_side = from_west(upwind)
    centre = upwind[..., 1:-1, :]
    left_cell = west_side[..., 1:-1, :]
    upper_row = upwind[..., 2:, :]
    upper_west = west_side[..., 2:, :]
    lower_row = upwind[..., :-2, :]
    lower_west = west_side[..., :-2, :]
    grad_lon = floored_ratio(centre - left_cell, jnp.abs(centre) + jnp.abs(left_cell))
    cross_lon = 0.5 * floored_ratio(
        upper_row + upper_west - lower_row - lower_west,
        jnp.abs(upper_row) + jnp.abs(upper_west) + jnp.abs(lower_row) + jnp.abs(lower_west),
    )
    speed_x = speed_lon[..., 2:-2, :]
    lat_west = from_west(speed_lat)
    mean_lat = 0.25 * (
        speed_lat[..., 2:-2, :]
        + speed_lat[..., 3:-1, :]
        + lat_west[..., 2:-2, :]
        + lat_west[..., 3:-1, :]
    )
    anti_lon = (jnp.abs(speed_x) - speed_x * speed_x) * grad_lon - speed_x * mean_lat * cross_lon
    above_row = upwind[..., 1:, :]
    below_row = upwind[..., :-1, :]
    grad_lat = floored_ratio(above_row - below_row, jnp.abs(above_row) + jnp.abs(below_row))
    above_east = from_east(above_row)
    below_east = from_east(below_row)
    above_west = from_west(above_row)
    below_west = from_west(below_row)
    cross_lat = 0.5 * floored_ratio(
        above_east + below_east - above_west - below_west,
        jnp.abs(above_east) + jnp.abs(below_east) + jnp.abs(above_west) + jnp.abs(below_west),
    )
    speed_y = speed_lat[..., 2:-1, :]
    lon_east = from_east(speed_lon)
    mean_lon = 0.25 * (
        speed_lon[..., 2:-1, :]
        + lon_east[..., 2:-1, :]
        + speed_lon[..., 1:-2, :]
        + lon_east[..., 1:-2, :]
    )
    anti_lat = (jnp.abs(speed_y) - speed_y * speed_y) * grad_lat - speed_y * mean_lon * cross_lat
    corr_lon = donor_flux(left_cell, centre, anti_lon)
    corr_lat = donor_flux(below_row, above_row, anti_lat)
    second = (
        centre - (from_east(corr_lon) - corr_lon) - (corr_lat[..., 1:, :] - corr_lat[..., :-1, :])
    )
    return jnp.where(inside[2:-2, None], second, 0.0)


def legendre_block(spectra, table_rows, pair_ids):
    degrees = spectra.shape[-1]
    lower_part = jnp.arange(degrees)[None, :] < (M - pair_ids)[:, None]
    nothing = jnp.zeros((), spectra.dtype)
    halves = jnp.stack(
        [jnp.where(lower_part, spectra, nothing), jnp.where(lower_part, nothing, spectra)], 0
    )
    return jnp.einsum("wrlsk,skt->swrlt", halves, table_rows, preferred_element_type=jnp.float32)


def angle_table(first_count, second_count, modulus):
    products = jnp.arange(first_count)[:, None] * jnp.arange(second_count)[None, :] % modulus
    return 2.0 * math.pi / modulus * products.astype(jnp.float32)


def fourier_rows(arrived, slot_pairs):
    positions = arrived.shape[0]
    row_count = arrived.shape[3] * arrived.shape[4]
    numbers = jnp.stack([slot_pairs, M - 1 - slot_pairs], 1).reshape(-1)
    sorting = jnp.argsort(numbers)
    spectrum = arrived.reshape(2 * positions, 2, row_count)[sorting].astype(jnp.float32)
    weights = jnp.where(jnp.arange(M) == 0, 1.0, 2.0).astype(jnp.float32)
    spectrum = spectrum * weights[:, None, None]
    real_part = spectrum[:, 0].reshape(M // FA, FA, row_count)
    imag_part = spectrum[:, 1].reshape(M // FA, FA, row_count)
    highest = lax.Precision.HIGHEST
    angle_one = angle_table(FB, M // FA, FB)
    cos_one = jnp.cos(angle_one)
    sin_one = jnp.sin(angle_one)
    mixed_real = jnp.einsum("am,mfx->afx", cos_one, real_part, precision=highest) - jnp.einsum(
        "am,mfx->afx", sin_one, imag_part, precision=highest
    )
    mixed_imag = jnp.einsum("am,mfx->afx", sin_one, real_part, precision=highest) + jnp.einsum(
        "am,mfx->afx", cos_one, imag_part, precision=highest
    )
    angle_two = angle_table(FB, FA, NLON)
    cos_two = jnp.cos(angle_two)[:, :, None]
    sin_two = jnp.sin(angle_two)[:, :, None]
    turned_real = mixed_real * cos_two - mixed_imag * sin_two
    turned_imag = mixed_real * sin_two + mixed_imag * cos_two
    angle_three = angle_table(FA, FA, FA)
    grid = jnp.einsum(
        "bf,afx->xba", jnp.cos(angle_three), turned_real, precision=highest
    ) - jnp.einsum("bf,afx->xba", jnp.sin(angle_three), turned_imag, precision=highest)
    return grid.reshape(arrived.shape[3], arrived.shape[4], NLON)


def body(spectral, legendre, wave_table, courant_lon, courant_lat):
    wave_count = lax.axis_size("wave")
    level_count = lax.axis_size("lev")
    wave_rank = lax.axis_index("wave")
    level_rank = lax.axis_index("lev")
    per_device = legendre.shape[0]
    own_start = (wave_rank * level_count + level_rank) * per_device
    own_pairs = lax.dynamic_slice_in_dim(wave_table, own_start, per_device)
    partial_terms = legendre_block(
        lax.all_to_all(spectral, "lev", split_axis=2, concat_axis=1, tiled=True),
        legendre,
        own_pairs,
    )
    coefficients = partial_terms.astype(jnp.bfloat16)
    arrived = lax.all_to_all(
        lax.all_to_all(coefficients, "wave", split_axis=4, concat_axis=0, tiled=True),
        "lev",
        split_axis=3,
        concat_axis=0,
        tiled=True,
    )
    slot_pairs = (
        wave_table.reshape(wave_count, level_count, per_device).transpose(1, 0, 2).reshape(-1)
    )
    tracer = fourier_rows(arrived, slot_pairs)
    lat_rows = tracer.shape[1]
    first_row = wave_rank * lat_rows
    window_rows = lat_rows * wave_count
    both_winds = jnp.stack([courant_lon, courant_lat], 0)
    wind_block = padded(both_winds, (("wave", 2),), 2)
    for number in range(PASSES):
        extended = padded(tracer, (("wave", 1),), 2)
        row_index = first_row + jnp.arange(-2, lat_rows + 2)
        tracer = mpdata_pass(
            extended, wind_block[0], wind_block[1], (row_index >= 0) & (row_index < window_rows)
        )
    return tracer


def solution(mesh):
    placed = (
        P(None, "lev", "wave", None),
        P(("wave", "lev"), None, None),
        P(),
        P("lev", "wave", None),
        P("lev", "wave", None),
    )
    return jax.shard_map(
        body, mesh=mesh, in_specs=placed, out_specs=P("lev", "wave", None), check_vma=False
    )
```

profile of v0, /device:TPU:32, one launch (start us, length us, event | category | flops | bytes accessed | tf_op | source)
XLA Modules:
  0.0 210.6 jit_solution(12310159613908070962)
XLA Ops:
  2.1 4.3 %all-to-all-start = ((bf16[2,4,20,1281]{3,1,0,2:T(4,128)(2,1)}), bf16[2,4,20,1281]{3,1,0,2:T(4,128)(2,1)}, u32[]{:S(2)}, u32[]{:S(2)}) async-start(bf16[2,4,20,1281]{3,1,0,2:T(4,128)(2,1)} %copy.26), calls=%async_computation | async-start | bytes 901120 | tf_op jit(solution)/shard_map/all_to_all | solution.py:158
  10.4 5.2 %collective-permute-start.3 = (f32[2,4,2,5120]{3,1,2,0:T(4,128)}, f32[2,4,2,5120]{3,1,2,0:T(4,128)}, u32[]{:S(2)}, u32[]{:S(2)}) collective-permute-start(f32[2,4,2,5120]{3,1,2,0:T(4,128)} %get-tuple-element.14), channel_id=1, source_target_pairs={{4,0},{8,4},{12,8},{16,12},{20,16},{24,20},{28,24},{32,28},{36,32}... | collective-permute-start | bytes 983048 | tf_op jit(solution)/shard_map/ppermute | solution.py:23
  20.3 5.0 %sort.17 = (s32[1280]{0:T(1024)}, s32[1280]{0:T(1024)S(1)}) sort(s32[1280]{0:T(1024)S(1)} %reshape.83, s32[1280]{0:T(1024)S(1)} %iota.56), dimensions={0}, to_apply=%region_0.1 | sort | flops 14080 | bytes 20480 | tf_op jit(solution)/shard_map/jit(argsort)/sort | solution.py:121
  34.6 10.3 %all-to-all-start.1 = ((bf16[32,2,1280]{2,1,0:T(2,128)(2,1)}), bf16[32,2,1280]{2,1,0:T(2,128)(2,1)S(1)}, u32[]{:S(2)}, u32[]{:S(2)}) async-start(bf16[32,2,1280]{2,1,0:T(2,128)(2,1)} %reshape.100), calls=%async_computation.1 | async-start | bytes 327680 | tf_op jit(solution)/shard_map/all_to_all | solution.py:164
  47.0 5.6 %all-to-all-done.1 = bf16[32,2,1280]{2,1,0:T(2,128)(2,1)S(1)} async-done(((bf16[32,2,1280]{2,1,0:T(2,128)(2,1)}), bf16[32,2,1280]{2,1,0:T(2,128)(2,1)S(1)}, u32[]{:S(2)}, u32[]{:S(2)}) %all-to-all-start.1) | async-done | bytes 163872 | tf_op jit(solution)/shard_map/all_to_all | solution.py:164
  56.6 16.6 %all-to-all-start.2 = ((bf16[160,2,2,16,8]{0,4,2,1,3:T(8,128)(2,1)}), bf16[160,2,2,16,8]{0,4,2,1,3:T(8,128)(2,1)S(1)}, u32[]{:S(2)}, u32[]{:S(2)}) async-start(bf16[160,2,2,16,8]{0,4,2,1,3:T(8,128)(2,1)} %copy.31), calls=%async_computation.2 | async-start | bytes 524288 | tf_op jit(solution)/shard_map/all_to_all | solution.py:163
  74.8 5.9 %all-to-all-done.2 = bf16[160,2,2,16,8]{0,4,2,1,3:T(8,128)(2,1)S(1)} async-done(((bf16[160,2,2,16,8]{0,4,2,1,3:T(8,128)(2,1)}), bf16[160,2,2,16,8]{0,4,2,1,3:T(8,128)(2,1)S(1)}, u32[]{:S(2)}, u32[]{:S(2)}) %all-to-all-start.2) | async-done | bytes 163872 | tf_op jit(solution)/shard_map/all_to_all | solution.py:163
  80.7 3.2 %copy.47 = bf16[4,160,2,2,4,8]{5,4,3,2,1,0:T(4,128)(2,1)} copy(bf16[4,160,2,2,4,8]{1,5,3,2,4,0:T(8,128)(2,1)S(1)} %bitcast.90) | data formatting | bytes 327680 | tf_op jit(solution)/shard_map/reshape | solution.py:122
  83.9 4.4 %reshape.99 = bf16[1280,2,32]{2,1,0:T(2,128)(2,1)S(1)} reshape(bf16[4,160,2,2,4,8]{5,4,3,2,1,0:T(4,128)(2,1)} %copy.47) | data formatting | bytes 327680 | tf_op jit(solution)/shard_map/reshape | solution.py:122
  88.2 4.4 %gather_fusion = bf16[1280,2,32]{2,1,0:T(2,128)(2,1)S(1)} fusion(bf16[1280,2,32]{2,1,0:T(2,128)(2,1)S(1)} %reshape.99, s32[2048]{0:T(1024)S(1)} %pad_clamp_fusion), kind=kCustom, calls=%fused_computation | custom fusion | bytes 332800 | tf_op jit(solution)/shard_map/gather | solution.py:122
  92.7 3.6 %convert_multiply_fusion = f32[1280,2,32]{2,1,0:T(2,128)S(1)} fusion(bf16[1280,2,32]{2,1,0:T(2,128)(2,1)S(1)} %gather_fusion, f32[1280]{0:T(1024)S(1)} %fusion.107), kind=kLoop, calls=%fused_computation.9 | loop fusion | flops 163840 | bytes 496640 | tf_op jit(solution)/shard_map/mul | solution.py:124
  98.4 2.8 %fusion.92 = f32[80,64,32]{0,1,2:T(8,128)} fusion(f32[20,64,32]{1,0,2:T(8,128)S(1)} %copy.48), kind=kOutput, calls=%fused_computation.210 | convolution fusion | flops 39336000 | bytes 819200 | tf_op jit(solution)/shard_map/am,mfx->afx/dot_general | solution.py:134
  104.4 3.1 %convolution_add_fusion = f32[80,64,32]{0,1,2:T(8,128)S(1)} fusion(f32[80,64,32]{0,1,2:T(8,128)} %fusion.92, f32[20,64,32]{1,0,2:T(8,128)S(1)} %copy.49), kind=kOutput, calls=%fused_computation.6 | convolution fusion | flops 39499840 | bytes 1474560 | tf_op jit(solution)/shard_map/am,mfx->afx/dot_general | solution.py:134
  118.5 6.4 %collective-permute-start.1 = (f32[4,2,5120]{2,0,1:T(4,128)S(1)}, f32[4,2,5120]{2,0,1:T(4,128)S(1)}, u32[]{:S(2)}, u32[]{:S(2)}) collective-permute-start(f32[4,2,5120]{2,0,1:T(4,128)S(1)} %copy.57), channel_id=1, source_target_pairs={{4,0},{8,4},{12,8},{16,12},{20,16},{24,20},{28,24},{32,28},{36,32}... | collective-permute-start | bytes 491528 | tf_op jit(solution)/shard_map/ppermute | solution.py:23
  134.0 3.9 %multiply_add_fusion.3 = (f32[4,9,5120]{2,0,1:T(4,128)S(1)}, f32[4,9,5120]{2,0,1:T(4,128)S(1)}) fusion(f32[4,9,5119]{2,0,1:T(4,128)S(1)} %get-tuple-element.44, f32[4,9,1]{2,0,1:T(4,128)S(1)} %get-tuple-element.48, f32[4,9,5119]{2,0,1:T(4,128)S(1)} %get-tuple-element.42, f32[4,9,1]{2,0,1:T(4,128)S(1)} %get-tuple-element.46, ...), kind=kLoop, calls=%fused_computation.113 | loop fusion | flops 7557120 | bytes 9093120 | tf_op jit(solution)/shard_map/add | solution.py:29
  138.4 7.4 %collective-permute-start.5 = (f32[4,2,5120]{2,0,1:T(4,128)S(1)}, f32[4,2,5120]{2,0,1:T(4,128)S(1)}, u32[]{:S(2)}, u32[]{:S(2)}) collective-permute-start(f32[4,2,5120]{2,0,1:T(4,128)S(1)} %get-tuple-element.54), channel_id=1, source_target_pairs={{4,0},{8,4},{12,8},{16,12},{20,16},{24,20},{28,24},{32,28},{36,32}... | collective-permute-start | bytes 491528 | tf_op jit(solution)/shard_map/ppermute | solution.py:23
  148.6 7.4 %collective-permute-done.4 = f32[4,2,5120]{2,0,1:T(4,128)S(1)} collective-permute-done((f32[4,2,5120]{2,0,1:T(4,128)S(1)}, f32[4,2,5120]{2,0,1:T(4,128)S(1)}, u32[]{:S(2)}, u32[]{:S(2)}) %collective-permute-start.4) | collective-permute-done | bytes 163872 | tf_op jit(solution)/shard_map/ppermute | solution.py:22
  162.3 2.8 %multiply_add_fusion.2 = f32[4,9,5120]{2,0,1:T(4,128)S(1)} fusion(f32[4,9,5120]{2,0,1:T(4,128)S(1)} %get-tuple-element.10, f32[4,9,5119]{2,0,1:T(4,128)S(1)} %get-tuple-element.36, f32[4,9,1]{2,0,1:T(4,128)S(1)} %get-tuple-element.40, f32[4,9,5119]{2,0,1:T(4,128)S(1)} %get-tuple-element.34, f32[4,9,1]{2,0,1:T(4,128)S(1)} %get-tuple-element.38, ...), kind=kLoop, calls=%fused_computation.111 | loop fusion | flops 6266880 | bytes 6635520 | tf_op jit(solution)/shard_map/add | solution.py:29
  167.6 4.1 %collective-permute-start.6 = (f32[4,2,5120]{2,0,1:T(4,128)S(1)}, f32[4,2,5120]{2,0,1:T(4,128)S(1)}, u32[]{:S(2)}, u32[]{:S(2)}) collective-permute-start(f32[4,2,5120]{2,0,1:T(4,128)S(1)} %get-tuple-element.51), channel_id=1, source_target_pairs={{0,4},{4,8},{8,12},{12,16},{16,20},{20,24},{24,28},{28,32},{32,36}... | collective-permute-start | bytes 491528 | tf_op jit(solution)/shard_map/ppermute | solution.py:22
  172.9 4.9 %collective-permute-done.6 = f32[4,2,5120]{2,0,1:T(4,128)S(1)} collective-permute-done((f32[4,2,5120]{2,0,1:T(4,128)S(1)}, f32[4,2,5120]{2,0,1:T(4,128)S(1)}, u32[]{:S(2)}, u32[]{:S(2)}) %collective-permute-start.6) | collective-permute-done | bytes 163872 | tf_op jit(solution)/shard_map/ppermute | solution.py:22
  184.1 2.8 %multiply_add_fusion.1 = f32[4,9,5120]{2,0,1:T(4,128)S(1)} fusion(f32[4,9,5120]{2,0,1:T(4,128)S(1)} %get-tuple-element.10, f32[4,9,5119]{2,0,1:T(4,128)S(1)} %get-tuple-element.28, f32[4,9,1]{2,0,1:T(4,128)S(1)} %get-tuple-element.32, f32[4,9,5119]{2,0,1:T(4,128)S(1)} %get-tuple-element.26, f32[4,9,1]{2,0,1:T(4,128)S(1)} %get-tuple-element.30, ...), kind=kLoop, calls=%fused_computation.109 | loop fusion | flops 6266880 | bytes 6635520 | tf_op jit(solution)/shard_map/add | solution.py:29
  189.3 4.1 %collective-permute-start.8 = (f32[4,2,5120]{2,0,1:T(4,128)S(1)}, f32[4,2,5120]{2,0,1:T(4,128)S(1)}, u32[]{:S(2)}, u32[]{:S(2)}) collective-permute-start(f32[4,2,5120]{2,0,1:T(4,128)S(1)} %get-tuple-element.49), channel_id=1, source_target_pairs={{0,4},{4,8},{8,12},{12,16},{16,20},{20,24},{24,28},{28,32},{32,36}... | collective-permute-start | bytes 491528 | tf_op jit(solution)/shard_map/ppermute | solution.py:22
  194.6 4.9 %collective-permute-done.8 = f32[4,2,5120]{2,0,1:T(4,128)S(1)} collective-permute-done((f32[4,2,5120]{2,0,1:T(4,128)S(1)}, f32[4,2,5120]{2,0,1:T(4,128)S(1)}, u32[]{:S(2)}, u32[]{:S(2)}) %collective-permute-start.8) | collective-permute-done | bytes 163872 | tf_op jit(solution)/shard_map/ppermute | solution.py:22
  205.8 2.9 %multiply_add_fusion = f32[4,9,5120]{2,0,1:T(4,128)S(1)} fusion(f32[4,9,5120]{2,0,1:T(4,128)S(1)} %get-tuple-element.10, f32[4,9,5119]{2,0,1:T(4,128)S(1)} %get-tuple-element.20, f32[4,9,1]{2,0,1:T(4,128)S(1)} %get-tuple-element.24, f32[4,9,5119]{2,0,1:T(4,128)S(1)} %get-tuple-element.18, f32[4,9,1]{2,0,1:T(4,128)S(1)} %get-tuple-element.22, ...), kind=kLoop, calls=%fused_computation.107 | loop fusion | flops 6266880 | bytes 6635520 | tf_op jit(solution)/shard_map/add | solution.py:29
  (145 shorter events, 83.3 us)
Async XLA Ops:
  0.0 30.5 %copy-start = (bf16[5,1281,256]{2,1,0:T(8,128)(2,1)S(1)}, bf16[5,1281,256]{2,1,0:T(8,128)(2,1)}, u32[]{:S(2)}) copy-start(bf16[5,1281,256]{2,1,0:T(8,128)(2,1)} %param.6) | copy-start | bytes 9838084
  2.1 23.3 %all-to-all-start = ((bf16[2,4,20,1281]{3,1,0,2:T(4,128)(2,1)}), bf16[2,4,20,1281]{3,1,0,2:T(4,128)(2,1)}, u32[]{:S(2)}, u32[]{:S(2)}) async-start(bf16[2,4,20,1281]{3,1,0,2:T(4,128)(2,1)} %copy.26), calls=%async_computation | async-start | bytes 901120 | tf_op jit(solution)/shard_map/all_to_all | solution.py:158
  6.4 11.2 %copy-start.11 = (s32[640]{0:T(1024)S(1)}, s32[640]{0:T(1024)}, u32[]{:S(2)}) copy-start(s32[640]{0:T(1024)} %param.7) | copy-start | bytes 7684
  8.5 0.8 copy-start.2
  8.5 1.8 copy-start.4
  10.4 62.8 %collective-permute-start.3 = (f32[2,4,2,5120]{3,1,2,0:T(4,128)}, f32[2,4,2,5120]{3,1,2,0:T(4,128)}, u32[]{:S(2)}, u32[]{:S(2)}) collective-permute-start(f32[2,4,2,5120]{3,1,2,0:T(4,128)} %get-tuple-element.14), channel_id=1, source_target_pairs={{4,0},{8,4},{12,8},{16,12},{20,16},{24,20},{28,24},{32,28},{36,32}... | collective-permute-start | bytes 983048 | tf_op jit(solution)/shard_map/ppermute | solution.py:23
  15.6 57.6 %collective-permute-start.2 = (f32[2,4,2,5120]{3,1,2,0:T(4,128)}, f32[2,4,2,5120]{3,1,2,0:T(4,128)}, u32[]{:S(2)}, u32[]{:S(2)}) collective-permute-start(f32[2,4,2,5120]{3,1,2,0:T(4,128)} %get-tuple-element.13), channel_id=1, source_target_pairs={{0,4},{4,8},{8,12},{12,16},{16,20},{20,24},{24,28},{28,32},{32,36}... | collective-permute-start | bytes 983048 | tf_op jit(solution)/shard_map/ppermute | solution.py:22
  34.6 18.0 %all-to-all-start.1 = ((bf16[32,2,1280]{2,1,0:T(2,128)(2,1)}), bf16[32,2,1280]{2,1,0:T(2,128)(2,1)S(1)}, u32[]{:S(2)}, u32[]{:S(2)}) async-start(bf16[32,2,1280]{2,1,0:T(2,128)(2,1)} %reshape.100), calls=%async_computation.1 | async-start | bytes 327680 | tf_op jit(solution)/shard_map/all_to_all | solution.py:164
  53.8 19.4 %copy-start.3 = (f32[1,4,8,5120]{3,1,2,0:T(4,128)S(1)}, f32[1,4,8,5120]{3,1,2,0:T(4,128)}, u32[]{:S(2)}) copy-start(f32[1,4,8,5120]{3,1,2,0:T(4,128)} %copy-done.2) | copy-start | bytes 1966084
  53.9 19.4 %copy-start.5 = (f32[1,4,8,5120]{3,1,2,0:T(4,128)S(1)}, f32[1,4,8,5120]{3,1,2,0:T(4,128)}, u32[]{:S(2)}) copy-start(f32[1,4,8,5120]{3,1,2,0:T(4,128)} %copy-done.4) | copy-start | bytes 1966084
  56.6 24.1 %all-to-all-start.2 = ((bf16[160,2,2,16,8]{0,4,2,1,3:T(8,128)(2,1)}), bf16[160,2,2,16,8]{0,4,2,1,3:T(8,128)(2,1)S(1)}, u32[]{:S(2)}, u32[]{:S(2)}) async-start(bf16[160,2,2,16,8]{0,4,2,1,3:T(8,128)(2,1)} %copy.31), calls=%async_computation.2 | async-start | bytes 524288 | tf_op jit(solution)/shard_map/all_to_all | solution.py:163
  104.4 4.9 %copy-start.7 = (f32[80,64]{0,1:T(8,128)S(1)}, f32[80,64]{0,1:T(8,128)}, u32[]{:S(2)}) copy-start(f32[80,64]{0,1:T(8,128)} %get-tuple-element.59) | copy-start | bytes 61444
  104.4 4.9 %copy-start.8 = (f32[80,64]{0,1:T(8,128)S(1)}, f32[80,64]{0,1:T(8,128)}, u32[]{:S(2)}) copy-start(f32[80,64]{0,1:T(8,128)} %get-tuple-element.60) | copy-start | bytes 61444
  114.9 10.5 %collective-permute-start = (f32[4,2,5120]{2,0,1:T(4,128)S(1)}, f32[4,2,5120]{2,0,1:T(4,128)S(1)}, u32[]{:S(2)}, u32[]{:S(2)}) collective-permute-start(f32[4,2,5120]{2,0,1:T(4,128)S(1)} %copy.56), channel_id=1, source_target_pairs={{0,4},{4,8},{8,12},{12,16},{16,20},{20,24},{24,28},{28,32},{32,36}... | collective-permute-start | bytes 491528 | tf_op jit(solution)/shard_map/ppermute | solution.py:22
  117.7 7.8 %copy-start.6 = (f32[4,8,5120]{2,1,0:T(8,128)S(1)}, f32[4,8,5120]{2,1,0:T(8,128)}, u32[]{:S(2)}) copy-start(f32[4,8,5120]{2,1,0:T(8,128)} %reshape.84) | copy-start | bytes 1966084
  118.5 9.1 %collective-permute-start.1 = (f32[4,2,5120]{2,0,1:T(4,128)S(1)}, f32[4,2,5120]{2,0,1:T(4,128)S(1)}, u32[]{:S(2)}, u32[]{:S(2)}) collective-permute-start(f32[4,2,5120]{2,0,1:T(4,128)S(1)} %copy.57), channel_id=1, source_target_pairs={{4,0},{8,4},{12,8},{16,12},{20,16},{24,20},{28,24},{32,28},{36,32}... | collective-permute-start | bytes 491528 | tf_op jit(solution)/shard_map/ppermute | solution.py:23
  134.0 3.9 %copy-start.9 = (pred[8]{0:T(512)(128)(4,1)S(1)}, pred[8]{0:T(512)(128)(4,1)}, u32[]{:S(2)}) copy-start(pred[8]{0:T(512)(128)(4,1)} %slice.578) | copy-start | bytes 28
  138.4 10.2 %collective-permute-start.5 = (f32[4,2,5120]{2,0,1:T(4,128)S(1)}, f32[4,2,5120]{2,0,1:T(4,128)S(1)}, u32[]{:S(2)}, u32[]{:S(2)}) collective-permute-start(f32[4,2,5120]{2,0,1:T(4,128)S(1)} %get-tuple-element.54), channel_id=1, source_target_pairs={{4,0},{8,4},{12,8},{16,12},{20,16},{24,20},{28,24},{32,28},{36,32}... | collective-permute-start | bytes 491528 | tf_op jit(solution)/shard_map/ppermute | solution.py:23
  145.8 10.2 %collective-permute-start.4 = (f32[4,2,5120]{2,0,1:T(4,128)S(1)}, f32[4,2,5120]{2,0,1:T(4,128)S(1)}, u32[]{:S(2)}, u32[]{:S(2)}) collective-permute-start(f32[4,2,5120]{2,0,1:T(4,128)S(1)} %get-tuple-element.53), channel_id=1, source_target_pairs={{0,4},{4,8},{8,12},{12,16},{16,20},{20,24},{24,28},{28,32},{32,36}... | collective-permute-start | bytes 491528 | tf_op jit(solution)/shard_map/ppermute | solution.py:22
  165.6 7.2 %collective-permute-start.7 = (f32[4,2,5120]{2,0,1:T(4,128)S(1)}, f32[4,2,5120]{2,0,1:T(4,128)S(1)}, u32[]{:S(2)}, u32[]{:S(2)}) collective-permute-start(f32[4,2,5120]{2,0,1:T(4,128)S(1)} %get-tuple-element.52), channel_id=1, source_target_pairs={{4,0},{8,4},{12,8},{16,12},{20,16},{24,20},{28,24},{32,28},{36,32}... | collective-permute-start | bytes 491528 | tf_op jit(solution)/shard_map/ppermute | solution.py:23
  167.6 10.2 %collective-permute-start.6 = (f32[4,2,5120]{2,0,1:T(4,128)S(1)}, f32[4,2,5120]{2,0,1:T(4,128)S(1)}, u32[]{:S(2)}, u32[]{:S(2)}) collective-permute-start(f32[4,2,5120]{2,0,1:T(4,128)S(1)} %get-tuple-element.51), channel_id=1, source_target_pairs={{0,4},{4,8},{8,12},{12,16},{16,20},{20,24},{24,28},{28,32},{32,36}... | collective-permute-start | bytes 491528 | tf_op jit(solution)/shard_map/ppermute | solution.py:22
  187.4 7.2 %collective-permute-start.9 = (f32[4,2,5120]{2,0,1:T(4,128)S(1)}, f32[4,2,5120]{2,0,1:T(4,128)S(1)}, u32[]{:S(2)}, u32[]{:S(2)}) collective-permute-start(f32[4,2,5120]{2,0,1:T(4,128)S(1)} %get-tuple-element.50), channel_id=1, source_target_pairs={{4,0},{8,4},{12,8},{16,12},{20,16},{24,20},{28,24},{32,28},{36,32}... | collective-permute-start | bytes 491528 | tf_op jit(solution)/shard_map/ppermute | solution.py:23
  189.3 10.2 %collective-permute-start.8 = (f32[4,2,5120]{2,0,1:T(4,128)S(1)}, f32[4,2,5120]{2,0,1:T(4,128)S(1)}, u32[]{:S(2)}, u32[]{:S(2)}) collective-permute-start(f32[4,2,5120]{2,0,1:T(4,128)S(1)} %get-tuple-element.49), channel_id=1, source_target_pairs={{0,4},{4,8},{8,12},{12,16},{16,20},{20,24},{24,28},{28,32},{32,36}... | collective-permute-start | bytes 491528 | tf_op jit(solution)/shard_map/ppermute | solution.py:22
  205.8 4.5 %copy-start.1 = (bf16[5,1281,256]{2,1,0:T(8,128)(2,1)S(1)}, bf16[5,1281,256]{2,1,0:T(8,128)(2,1)}, u32[]{:S(2)}) copy-start(bf16[5,1281,256]{2,1,0:T(8,128)(2,1)} %param.6) | copy-start | bytes 9838084
  (1 other events, 0.7 us)
where the time goes:
time: 213 us; the launch traced here: 211 us
  starting transfers between devices  69.2 us (32%)
  local copies, waits for them, and re-layouts  50.2 us (24%)
  other arithmetic  43.5 us (20%)
  waiting for transfers between devices  33.7 us (16%)
  matrix products  12.8 us (6%)
    add x16, other arithmetic, donor_flux(): jnp.maximum(speed, 0.0) * left_side + jnp.minimum(speed, 0.0) * right_side  25.2 us
    ppermute x5, starting transfers between devices, padded(): after = lax.ppermute(initial, axis, down)  22.9 us
    ppermute x5, waiting for transfers between devices, padded(): before = lax.ppermute(last, axis, up)  17.8 us
    all_to_all x1, starting transfers between devices, body(): lax.all_to_all(lax.all_to_all(coefficients, 'wave', split_axis=4, concat_...  16.6 us
    ppermute x5, starting transfers between devices, padded(): before = lax.ppermute(last, axis, up)  15.1 us
    all_to_all x1, starting transfers between devices, body(): lax.all_to_all(coefficients, 'wave', split_axis=4, concat_axis=0, tiled=T...  10.3 us
    slice x26, local copies, waits for them, and re-layouts, from_east(): return jnp.roll(field, -1, axis=-1)  8.87 us
    reshape x2, local copies, waits for them, and re-layouts, fourier_rows(): arrived.reshape(2 * positions, 2, row_count)[sorting].astype(jnp.float32)  7.54 us
  transfers between devices with their start and end apart: 13, of which 10 were waited for; matrix products, arithmetic and copies ran while one was open for 13% of the time, Pallas kernels for 0%

commit v1 on v0

v1 whole, which is shorter than its diff:
```python
import math

import jax
import jax.numpy as jnp
import numpy as np
from jax import lax
from jax.experimental import pallas as pl
from jax.experimental.pallas import tpu as pltpu
from jax.sharding import PartitionSpec as P

M = 1280
NLON = 5120
K = 1281
PASSES = 4
WAVES = 32
LEVS = 4
SLOTS = 5
ROWS = 8
NF = 40
NB = 128
F32 = jnp.float32
BF16 = jnp.bfloat16
MESH = pl.DeviceIdType.MESH


def split_table(values):
    high = values.astype(np.float32).astype(BF16)
    low = (values - high.astype(np.float64)).astype(np.float32).astype(BF16)
    return high, low


def first_stage_tables():
    g = np.arange(5)[:, None, None, None]
    h = np.arange(2)[None, :, None, None]
    f8 = np.arange(8)[None, None, :, None]
    p1 = np.arange(16)[None, None, None, :]
    m = np.where(h == 0, 40 * p1 + 8 * g + f8, M - 1 - (40 * p1 + 8 * (4 - g) + f8))
    m = m.reshape(5, 256, 1)
    angle = 2.0 * math.pi / NLON * ((m * np.arange(NB)[None, None, :]) % NLON)
    weight = np.where(m == 0, 1.0, 2.0)
    return split_table(np.concatenate([weight * np.cos(angle), weight * np.sin(angle)], -1))


def second_stage_table():
    row = np.arange(NF)
    place = 5 * (row % 8) + row // 8
    angle = 2.0 * math.pi / NF * ((place[:, None] * np.arange(NF)[None, :]) % NF)
    high, low = split_table(np.concatenate([np.cos(angle), -np.sin(angle)], -1))
    return np.concatenate([high, low, high], -1)


def pack_table():
    t8 = np.arange(8)[:, None, None]
    lane = np.arange(128)[None, :, None]
    h, v, c, l = lane // 32, lane // 8 % 4, lane // 4 % 2, lane % 4
    goal = v * 128 + h * 64 + c * 32 + t8 * 4 + l
    hit = (goal == np.arange(512)[None, None, :]) & (lane < 64)
    return hit.astype(np.float32).astype(BF16)


def dot(a, b):
    return jnp.dot(a, b, preferred_element_type=F32)


def legendre_kernel(pairs_ref, x_ref, leg_ref, pack_ref, msg_ref, turned, lined):
    lined[...] = jnp.zeros_like(lined)
    lane = lax.broadcasted_iota(jnp.int32, (1, K), 1)
    for s in range(SLOTS):
        low = lane < (M - pairs_ref[s])
        spectra = x_ref[:, s].reshape(32, K)
        zero = jnp.zeros_like(spectra)
        halves = jnp.concatenate(
            [jnp.where(low, spectra, zero), jnp.where(low, zero, spectra)], 0
        )
        total = dot(halves[:, : K - 1], leg_ref[s, : K - 1, :])
        last = spectra[:, K - 1 : K].astype(F32) * leg_ref[s, K - 1 : K, :].astype(F32)
        total = jnp.concatenate([total[:32], total[32:] + last], 0)
        rounded = total.astype(BF16).astype(F32)
        square = jnp.concatenate([rounded, jnp.zeros_like(rounded)], 0)
        turned[...] = square.T
        for t8 in range(8):
            lined[t8, pl.ds(s, WAVES, stride=8), :] = turned[pl.ds(t8, WAVES, stride=8), :]
    total = dot(lined[0].astype(BF16), pack_ref[0])
    for t8 in range(1, 8):
        total += dot(lined[t8].astype(BF16), pack_ref[t8])
    packed = total.astype(BF16)
    for v in range(LEVS):
        msg_ref[:, v] = packed[:, v * 128 : (v + 1) * 128].reshape(WAVES, 8, 128)


def west(v, edge):
    r = pltpu.roll(v, 1, 1)
    before = jnp.concatenate([pltpu.roll(r[32:40], 1, 0), r[0:32]], 0)
    return jnp.where(edge, before, r)


def east(v, edge):
    r = pltpu.roll(v, 127, 1)
    after = jnp.concatenate([r[8:40], pltpu.roll(r[0:8], 7, 0)], 0)
    return jnp.where(edge, after, r)


def ratio(x, y):
    return x / jnp.maximum(y, 1.0)


def advance_kernel(
    tbl_ref, recv_ref, hi_ref, lo_ref, two_ref, lon_ref, lat_ref, out_ref,
    qt, ast, fld, cx, cy, cxp, cxm, cyp, cym, ax, bx, ay, by,
    q1s, wst, swe, awe, dew, aew, gys, stage, halo,
    csend, crecv, hsend, hrecv,
):
    me = lax.axis_index("wave")
    up = lax.rem(me + 1, WAVES)
    down = lax.rem(me + WAVES - 1, WAVES)
    has_up = me < WAVES - 1
    has_down = me > 0

    barrier = pltpu.get_barrier_semaphore()
    for nb in (up, down):
        pl.semaphore_signal(barrier, inc=1, device_id={"wave": nb}, device_id_type=MESH)
    pl.semaphore_wait(barrier, 2)

    def remote(src, dst, ssem, rsem, nb):
        return pltpu.make_async_remote_copy(
            src_ref=src, dst_ref=dst, send_sem=ssem, recv_sem=rsem,
            device_id={"wave": nb}, device_id_type=MESH,
        )

    def repack(l, carry):
        for i in range(ROWS):
            for k in range(5):
                cx[i + 1, l, 8 * k : 8 * k + 8, :] = lon_ref[l, pl.ds(8 * k + i, 8, stride=40), :]
                cy[i + 1, l, 8 * k : 8 * k + 8, :] = lat_ref[l, pl.ds(8 * k + i, 8, stride=40), :]
        return carry

    lax.fori_loop(0, LEVS, repack, 0)
    courant = [
        remote(cx.at[8], cx.at[0], csend.at[0], crecv.at[0], up),
        remote(cy.at[8], cy.at[0], csend.at[1], crecv.at[1], up),
        remote(cx.at[1], cx.at[9], csend.at[2], crecv.at[2], down),
        remote(cy.at[pl.ds(1, 2)], cy.at[pl.ds(9, 2)], csend.at[3], crecv.at[3], down),
    ]
    for c in courant:
        c.start()

    row = lax.broadcasted_iota(jnp.int32, (640, 1), 0)
    pair_of = 40 * (row % 16) + 8 * (row // 128) + row // 16 % 8
    choose = jnp.where(tbl_ref[...] == pair_of, 1.0, 0.0).astype(BF16)
    ordered = dot(choose, recv_ref[...])
    for g in range(5):
        qt[g] = ordered[g * 128 : (g + 1) * 128, :].T

    lane = lax.broadcasted_iota(jnp.int32, (8, 128), 1)
    sub = lax.broadcasted_iota(jnp.int32, (8, 128), 0)
    masks = (lane // 16 == sub, lane // 16 == 7 - sub)

    def first(g, carry):
        total = None
        for h in range(2):
            source = g if h == 0 else 4 - g
            rows = slice(h * 128, h * 128 + 128)
            th, tl = hi_ref[g, rows, :], lo_ref[g, rows, :]
            for c in range(2):
                blocks = []
                for x in range(32):
                    line = qt[source, pl.ds(h * 64 + c * 32 + x, 8, stride=0), :]
                    blocks.append(jnp.where(masks[h], line, 0.0))
                lhs = jnp.concatenate(blocks, 0).astype(BF16)
                for table in (th, tl):
                    if c == 1:
                        table = jnp.concatenate([-table[:, 128:], table[:, :128]], 1)
                    term = dot(lhs, table)
                    total = term if total is None else total + term
        total = total.reshape(32, 8, 256)
        at = pl.multiple_of(8 * g, 8)
        ast[:, 0, pl.ds(at, 8), :] = total[:, :, :128]
        ast[:, 1, pl.ds(at, 8), :] = total[:, :, 128:]
        return carry

    lax.fori_loop(0, 5, first, 0)

    def halo_copies(parity, l):
        return [
            remote(stage.at[parity, 1, l], halo.at[parity, 0, l],
                   hsend.at[parity, 0, l], hrecv.at[parity, 0, l], up),
            remote(stage.at[parity, 0, l], halo.at[parity, 1, l],
                   hsend.at[parity, 1, l], hrecv.at[parity, 1, l], down),
        ]

    def send_halo(parity, l):
        for i in range(2):
            stage[parity, 0, l, i] = fld[2 + i, l].astype(BF16)
            stage[parity, 1, l, i] = fld[8 + i, l].astype(BF16)
        for c in halo_copies(parity, l):
            c.start()

    def second(l, carry):
        for t in range(0, ROWS, 2):
            parts = []
            for u in (t, t + 1):
                both = ast[u * 4 + l].reshape(80, 128)
                high = both.astype(BF16)
                low = (both - high.astype(F32)).astype(BF16)
                parts.append(jnp.concatenate([high, high, low], 0))
            values = dot(two_ref[...], jnp.concatenate(parts, 1))
            fld[2 + t, l] = values[:, :128]
            fld[3 + t, l] = values[:, 128:]
        send_halo(0, l)
        return carry

    lax.fori_loop(0, LEVS, second, 0)

    for c in courant:
        c.wait()
    lanes = lax.broadcasted_iota(jnp.int32, (NF, 128), 1)
    first_lane = lanes == 0
    last_lane = lanes == 127

    def terms(l, carry):
        zero = jnp.zeros((NF, 128), F32)
        cx[0, l] = jnp.where(has_down, cx[0, l], zero)
        cy[0, l] = jnp.where(has_down, cy[0, l], zero)
        cx[9, l] = jnp.where(has_up, cx[9, l], zero)
        cy[9, l] = jnp.where(has_up, cy[9, l], zero)
        cy[10, l] = jnp.where(has_up, cy[10, l], zero)
        for r in range(11):
            v = cy[r, l]
            cyp[r, l] = jnp.maximum(v, 0.0)
            cym[r, l] = jnp.minimum(v, 0.0)
            if r < 10:
                u = cx[r, l]
                cxp[r, l] = jnp.maximum(u, 0.0)
                cxm[r, l] = jnp.minimum(u, 0.0)
        for i in range(ROWS):
            u = cx[i + 1, l]
            ax[i, l] = jnp.abs(u) - u * u
            pair = cy[i + 1, l] + cy[i + 2, l]
            bx[i, l] = (u * 0.125) * (pair + west(pair, first_lane))
        for i in range(ROWS + 1):
            v = cy[i + 1, l]
            ay[i, l] = jnp.abs(v) - v * v
            pair = cx[i + 1, l] + cx[i, l]
            by[i, l] = (v * 0.125) * (pair + east(pair, last_lane))
        return carry

    lax.fori_loop(0, LEVS, terms, 0)

    def level_pass(step, carry):
        number = step // LEVS
        l = step % LEVS
        parity = number % 2
        for c in halo_copies(parity, l):
            c.wait()
        zero = jnp.zeros((NF, 128), F32)
        for i in range(2):
            fld[i, l] = jnp.where(has_down, halo[parity, 0, l, i].astype(F32), zero)
            fld[10 + i, l] = jnp.where(has_up, halo[parity, 1, l, i].astype(F32), zero)
        flux = None
        for r in range(-1, 9):
            q = fld[r + 2, l]
            if flux is None:
                flux = cyp[r + 1, l] * fld[r + 1, l] + cym[r + 1, l] * q
            above = cyp[r + 2, l] * q + cym[r + 2, l] * fld[r + 3, l]
            fx = cxp[r + 1, l] * west(q, first_lane) + cxm[r + 1, l] * q
            v = q - (east(fx, last_lane) - fx) - (above - flux)
            flux = above
            if r == -1:
                v = jnp.where(has_down, v, zero)
            if r == 8:
                v = jnp.where(has_up, v, zero)
            w = west(v, first_lane)
            e = east(v, last_lane)
            aw = jnp.abs(w)
            q1s[r + 1] = v
            wst[r + 1] = w
            swe[r + 1] = v + w
            awe[r + 1] = jnp.abs(v) + aw
            dew[r + 1] = e - w
            aew[r + 1] = jnp.abs(e) + aw

        def face(i):
            a, b = q1s[i + 1], q1s[i]
            grad = ratio(a - b, jnp.abs(a) + jnp.abs(b))
            cross = ratio(dew[i + 1] + dew[i], aew[i + 1] + aew[i])
            vy = ay[i, l] * grad - by[i, l] * cross
            gys[i] = jnp.maximum(vy, 0.0) * b + jnp.minimum(vy, 0.0) * a

        def finish(i):
            v, w = q1s[i + 1], wst[i + 1]
            grad = ratio(v - w, awe[i + 1])
            cross = ratio(swe[i + 2] - swe[i], awe[i + 2] + awe[i])
            vx = ax[i, l] * grad - bx[i, l] * cross
            gx = jnp.maximum(vx, 0.0) * w + jnp.minimum(vx, 0.0) * v
            fld[i + 2, l] = v - (east(gx, last_lane) - gx) - (gys[i + 1] - gys[i])

        for i in (0, 1, 2):
            face(i)
        for i in (0, 1):
            finish(i)
        for i in (6, 7, 8):
            face(i)
        for i in (6, 7):
            finish(i)

        @pl.when(number < PASSES - 1)
        def _():
            send_halo(1 - parity, l)

        for i in (3, 4, 5):
            face(i)
        for i in (2, 3, 4, 5):
            finish(i)
        return carry

    lax.fori_loop(0, PASSES * LEVS, level_pass, 0)

    def deliver(l, carry):
        for i in range(ROWS):
            for k in range(5):
                out_ref[l, pl.ds(8 * k + i, 8, stride=40), :] = fld[i + 2, l, 8 * k : 8 * k + 8, :]
        return carry

    lax.fori_loop(0, LEVS, deliver, 0)


def tiles_of(winds):
    return winds.reshape(LEVS, ROWS, NF, NB).transpose(0, 2, 1, 3).reshape(LEVS, NF * ROWS, NB)


def body(spectral, legendre, wave_table, courant_lon, courant_lat):
    wave_rank = lax.axis_index("wave")
    level_rank = lax.axis_index("lev")
    own_pairs = lax.dynamic_slice_in_dim(
        wave_table, (wave_rank * LEVS + level_rank) * SLOTS, SLOTS
    )
    table = jnp.pad(wave_table.reshape(128, SLOTS), ((0, 0), (0, 3)), constant_values=-1)
    table = table.reshape(1, 1024)
    parts = spectral.reshape(2, 4, LEVS, SLOTS, K).transpose(2, 3, 0, 1, 4)
    parts = parts.reshape(LEVS, SLOTS, 8, K)
    arrived = lax.all_to_all(parts, "lev", split_axis=0, concat_axis=0, tiled=True)

    vmem = pl.BlockSpec(memory_space=pltpu.VMEM)
    smem = pl.BlockSpec(memory_space=pltpu.SMEM)
    messages = pl.pallas_call(
        legendre_kernel,
        out_shape=jax.ShapeDtypeStruct((WAVES, LEVS, 8, 128), BF16),
        in_specs=[smem, vmem, vmem, vmem],
        out_specs=vmem,
        scratch_shapes=[
            pltpu.VMEM((256, 128), F32),
            pltpu.VMEM((8, 256, 128), F32),
        ],
        name="legendre",
    )(own_pairs, arrived, legendre, jnp.asarray(pack_table()))
    received = lax.all_to_all(
        messages.reshape(128, 8, 128), ("wave", "lev"), split_axis=0, concat_axis=0, tiled=True
    )
    high, low = first_stage_tables()
    big = lambda rows: pltpu.VMEM((rows, LEVS, NF, NB), F32)
    small = lambda rows: pltpu.VMEM((rows, NF, NB), F32)
    out = pl.pallas_call(
        advance_kernel,
        out_shape=jax.ShapeDtypeStruct((LEVS, NF * ROWS, NB), F32),
        in_specs=[vmem] * 7,
        out_specs=vmem,
        scratch_shapes=[
            pltpu.VMEM((5, 128, 128), F32),
            pltpu.VMEM((32, 2, NF, NB), F32),
            big(12), big(10), big(11), big(10), big(10), big(11), big(11),
            big(8), big(8), big(9), big(9),
            small(10), small(10), small(10), small(10), small(10), small(10), small(9),
            pltpu.VMEM((2, 2, LEVS, 2, NF, NB), BF16),
            pltpu.VMEM((2, 2, LEVS, 2, NF, NB), BF16),
            pltpu.SemaphoreType.DMA((4,)),
            pltpu.SemaphoreType.DMA((4,)),
            pltpu.SemaphoreType.DMA((2, 2, LEVS)),
            pltpu.SemaphoreType.DMA((2, 2, LEVS)),
        ],
        compiler_params=pltpu.CompilerParams(collective_id=0, has_side_effects=True),
        name="advance",
    )(
        table, received.reshape(1024, 128), jnp.asarray(high), jnp.asarray(low),
        jnp.asarray(second_stage_table()), tiles_of(courant_lon), tiles_of(courant_lat),
    )
    out = out.reshape(LEVS, NF, ROWS, NB).transpose(0, 2, 1, 3)
    return out.reshape(LEVS, ROWS, NLON)


def solution(mesh):
    placed = (
        P(None, "lev", "wave", None),
        P(("wave", "lev"), None, None),
        P(),
        P("lev", "wave", None),
        P("lev", "wave", None),
    )
    return jax.shard_map(
        body, mesh=mesh, in_specs=placed, out_specs=P("lev", "wave", None), check_vma=False
    )
```

time: 213 us -> 78.4 us (0.37)
  the two profiles are of different devices: /device:TPU:32 before, /device:TPU:0 now
where the time goes in v1:
time: 78.4 us; the launch traced here: 78 us
  Pallas kernels  38.8 us (49%)
  waiting for transfers between devices  18.1 us (23%)
  starting transfers between devices  13.2 us (17%)
  local copies, waits for them, and re-layouts  7.77 us (10%)
    pallas_call x1, Pallas kernels, body(): pl.pallas_call(advance_kernel, out_shape=jax.ShapeDtypeStruct((LEVS, NF *...  34 us
    all_to_all x1, waiting for transfers between devices, body(): lax.all_to_all(messages.reshape(128, 8, 128), ('wave', 'lev'), split_axis...  9.92 us
    all_to_all x1, starting transfers between devices, body(): lax.all_to_all(messages.reshape(128, 8, 128), ('wave', 'lev'), split_axis...  8.67 us
    all_to_all x1, waiting for transfers between devices, body(): lax.all_to_all(parts, 'lev', split_axis=0, concat_axis=0, tiled=True)  8.23 us
    pallas_call x1, Pallas kernels, body(): pl.pallas_call(legendre_kernel, out_shape=jax.ShapeDtypeStruct((WAVES, LE...  4.78 us
    all_to_all x1, starting transfers between devices, body(): lax.all_to_all(parts, 'lev', split_axis=0, concat_axis=0, tiled=True)  4.54 us
    unnamed x7, local copies, waits for them, and re-layouts  3.44 us
  transfers between devices with their start and end apart: 2, of which 2 were waited for; matrix products, arithmetic and copies ran while one was open for 3% of the time, Pallas kernels for 0%

profile of v1, /device:TPU:0, one launch (start us, length us, event | category | flops | bytes accessed | tf_op | source)
XLA Modules:
  0.0 78.0 jit_solution(1976034969797067840)
XLA Ops:
  0.0 1.2 %copy.13 = bf16[2,4,4,5,1281]{4,1,0,3,2:T(4,128)(2,1)S(1)} copy(bf16[2,4,4,5,1281]{4,1,3,2,0:T(4,128)(2,1)} %bitcast.27) | data formatting | bytes 819840 | tf_op jit(solution)/shard_map/reshape | solution.py:339
  1.2 1.0 %reshape.39 = bf16[4,5,8,1281]{3,2,1,0:T(8,128)(2,1)} reshape(bf16[4,5,2,4,1281]{4,3,2,1,0:T(4,128)(2,1)S(1)} %bitcast.22) | data formatting | bytes 819840 | tf_op jit(solution)/shard_map/reshape | solution.py:340
  2.1 0.0 copy-start.2
  2.2 4.5 %all-to-all-start = ((bf16[4,5,8,1281]{3,2,1,0:T(8,128)(2,1)}), bf16[4,5,8,1281]{3,2,1,0:T(8,128)(2,1)S(1)}, u32[]{:S(2)}, u32[]{:S(2)}) async-start(bf16[4,5,8,1281]{3,2,1,0:T(8,128)(2,1)} %reshape.39), calls=%async_computation | async-start | bytes 901120 | tf_op jit(solution)/shard_map/all_to_all | solution.py:341
  6.7 1.3 %dynamic_slice.3.pairs_ref = s32[5]{0:T(128)} dynamic-slice(s32[640]{0:T(1024)} %param.11, s32[]{:T(128)S(6)} %select_n.3), dynamic_slice_sizes={5} | dynamic-slice | bytes 44 | tf_op jit(solution)/shard_map/dynamic_slice | solution.py:334
  8.0 8.2 %all-to-all-done.x_ref = bf16[4,5,8,1281]{3,2,1,0:T(8,128)(2,1)S(1)} async-done(((bf16[4,5,8,1281]{3,2,1,0:T(8,128)(2,1)}), bf16[4,5,8,1281]{3,2,1,0:T(8,128)(2,1)S(1)}, u32[]{:S(2)}, u32[]{:S(2)}) %all-to-all-start) | async-done | bytes 409952 | tf_op jit(solution)/shard_map/all_to_all | solution.py:341
  16.2 0.0 copy-start
  16.2 0.8 copy-done
  17.0 4.8 %legendre.1 = bf16[32,4,8,128]{3,2,1,0:T(8,128)(2,1)} custom-call(s32[5]{0:T(128)} %dynamic_slice.3.pairs_ref, bf16[4,5,8,1281]{3,2,1,0:T(8,128)(2,1)} %copy-done, bf16[5,1281,256]{2,1,0:T(8,128)(2,1)} %leg_ref.1, bf16[8,128,512]{2,1,0:T(8,128)(2,1)} %constant.27.clone.pack_ref), custom_call_target="tpu_custom_call" | custom-call | tf_op jit(solution)/shard_map/legendre/pallas_call | solution.py:345
  21.8 8.7 %all-to-all-start.1 = ((bf16[128,8,128]{2,1,0:T(8,128)(2,1)}), bf16[128,8,128]{2,1,0:T(8,128)(2,1)S(1)}, u32[]{:S(2)}, u32[]{:S(2)}) async-start(bf16[128,8,128]{2,1,0:T(8,128)(2,1)} %bitcast.24), calls=%async_computation.1 | async-start | bytes 524288 | tf_op jit(solution)/shard_map/all_to_all | solution.py:356
  30.4 0.0 copy-done.2
  30.5 0.2 reshape.36
  30.7 0.7 reshape.37.tbl_ref
  31.4 9.9 %all-to-all-done.1 = bf16[128,8,128]{2,1,0:T(8,128)(2,1)S(1)} async-done(((bf16[128,8,128]{2,1,0:T(8,128)(2,1)}), bf16[128,8,128]{2,1,0:T(8,128)(2,1)S(1)}, u32[]{:S(2)}, u32[]{:S(2)}) %all-to-all-start.1) | async-done | bytes 262176 | tf_op jit(solution)/shard_map/all_to_all | solution.py:356
  41.3 0.0 copy-start.1
  41.3 0.7 copy-done.1
  42.0 34.0 %advance.1 = f32[4,320,128]{2,1,0:T(8,128)} custom-call(s32[1,1024]{1,0:T(1,128)} %reshape.37.tbl_ref, bf16[1024,128]{1,0:T(8,128)(2,1)} %bitcast.23, bf16[5,256,256]{2,1,0:T(8,128)(2,1)} %constant.28.clone.hi_ref, bf16[5,256,256]{2,1,0:T(8,128)(2,1)} %constant.29.clone.lo_ref, bf16[40,240]{1,0:T(8,128)(2,1)} %constant.30.clone.two_ref, ...), custom_call_target="tpu_custom_call" | custom-call | tf_op jit(solution)/shard_map/advance/pallas_call | solution.py:362
  76.0 2.0 %copy.15 = f32[4,8,5120]{2,1,0:T(8,128)} copy(f32[4,8,5120]{2,1,0:T(8,128)} %bitcast.21) | data formatting | bytes 1310720
  (1 shorter events, 0.0 us)
Async XLA Ops:
  2.1 28.3 %copy-start.2 = (s32[640]{0:T(1024)S(1)}, s32[640]{0:T(1024)}, u32[]{:S(2)}) copy-start(s32[640]{0:T(1024)} %param.11) | copy-start | bytes 7684
  2.2 14.1 %all-to-all-start = ((bf16[4,5,8,1281]{3,2,1,0:T(8,128)(2,1)}), bf16[4,5,8,1281]{3,2,1,0:T(8,128)(2,1)S(1)}, u32[]{:S(2)}, u32[]{:S(2)}) async-start(bf16[4,5,8,1281]{3,2,1,0:T(8,128)(2,1)} %reshape.39), calls=%async_computation | async-start | bytes 901120 | tf_op jit(solution)/shard_map/all_to_all | solution.py:341
  16.2 0.8 copy-start
  21.8 19.5 %all-to-all-start.1 = ((bf16[128,8,128]{2,1,0:T(8,128)(2,1)}), bf16[128,8,128]{2,1,0:T(8,128)(2,1)S(1)}, u32[]{:S(2)}, u32[]{:S(2)}) async-start(bf16[128,8,128]{2,1,0:T(8,128)(2,1)} %bitcast.24), calls=%async_computation.1 | async-start | bytes 524288 | tf_op jit(solution)/shard_map/all_to_all | solution.py:356
  41.3 0.7 copy-start.1

commit v2 on v1

v2 whole, which is shorter than its diff:
```python
import math

import jax
import jax.numpy as jnp
import numpy as np
from jax import lax
from jax.experimental import pallas as pl
from jax.experimental.pallas import tpu as pltpu
from jax.sharding import PartitionSpec as P

M = 1280
NLON = 5120
K = 1281
PASSES = 4
WAVES = 32
LEVS = 4
SLOTS = 5
ROWS = 8
NF = 40
NB = 128
F32 = jnp.float32
BF16 = jnp.bfloat16
MESH = pl.DeviceIdType.MESH


def split_table(values):
    high = values.astype(np.float32).astype(BF16)
    low = (values - high.astype(np.float64)).astype(np.float32).astype(BF16)
    return high, low


def first_stage_tables():
    g = np.arange(5)[:, None, None, None]
    h = np.arange(2)[None, :, None, None]
    f8 = np.arange(8)[None, None, :, None]
    p1 = np.arange(16)[None, None, None, :]
    m = np.where(h == 0, 40 * p1 + 8 * g + f8, M - 1 - (40 * p1 + 8 * (4 - g) + f8))
    m = m.reshape(5, 256, 1)
    angle = 2.0 * math.pi / NLON * ((m * np.arange(NB)[None, None, :]) % NLON)
    weight = np.where(m == 0, 1.0, 2.0)
    return split_table(np.concatenate([weight * np.cos(angle), weight * np.sin(angle)], -1))


def second_stage_table():
    row = np.arange(NF)
    place = 5 * (row % 8) + row // 8
    angle = 2.0 * math.pi / NF * ((place[:, None] * np.arange(NF)[None, :]) % NF)
    high, low = split_table(np.concatenate([np.cos(angle), -np.sin(angle)], -1))
    return np.concatenate([high, low, high], -1)


def pack_table():
    t8 = np.arange(8)[:, None, None]
    lane = np.arange(128)[None, :, None]
    h, v, c, l = lane // 32, lane // 8 % 4, lane // 4 % 2, lane % 4
    goal = v * 128 + h * 64 + c * 32 + t8 * 4 + l
    hit = (goal == np.arange(512)[None, None, :]) & (lane < 64)
    return hit.astype(np.float32).astype(BF16)


def dot(a, b):
    return jnp.dot(a, b, preferred_element_type=F32)


def west(v, edge):
    r = pltpu.roll(v, 1, 1)
    before = jnp.concatenate([pltpu.roll(r[32:40], 1, 0), r[0:32]], 0)
    return jnp.where(edge, before, r)


def east(v, edge):
    r = pltpu.roll(v, 127, 1)
    after = jnp.concatenate([r[8:40], pltpu.roll(r[0:8], 7, 0)], 0)
    return jnp.where(edge, after, r)


def ratio(x, y):
    return x / jnp.maximum(y, 1.0)


def whole_kernel(
    pairs_ref, tbl_ref, spec_hbm, leg_hbm, lon_hbm, lat_hbm, pack_hbm, hi_hbm, lo_hbm, two_hbm,
    out_ref,
    leg_ref, lon_ref, lat_ref, pack_ref, hi_ref, lo_ref, two_ref,
    arrived, turned, lined, msgs, recv, choose,
    qt, ast, fld, cx, cy, cxp, cxm, cyp, cym, ax, bx, ay, by,
    q1s, wst, swe, awe, dew, aew, gys, stage, halo,
    lsem, ssend, srecv, asend, arecv, csend, crecv, hsend, hrecv,
):
    me = lax.axis_index("wave")
    lev = lax.axis_index("lev")
    rank = me * LEVS + lev
    up = lax.rem(me + 1, WAVES)
    down = lax.rem(me + WAVES - 1, WAVES)
    has_up = me < WAVES - 1
    has_down = me > 0

    barrier = pltpu.get_barrier_semaphore()

    def greet(step, carry):
        peer = lax.rem(rank + step, 128)
        pl.semaphore_signal(
            barrier, inc=1, device_id={"wave": peer // LEVS, "lev": peer % LEVS},
            device_id_type=MESH,
        )
        return carry

    lax.fori_loop(1, 128, greet, 0)

    local = [
        pltpu.make_async_copy(a, b, lsem.at[n])
        for n, (a, b) in enumerate(
            [(lon_hbm, lon_ref), (lat_hbm, lat_ref), (leg_hbm, leg_ref), (pack_hbm, pack_ref),
             (hi_hbm, hi_ref), (lo_hbm, lo_ref), (two_hbm, two_ref)]
        )
    ]
    own = pltpu.make_async_copy(
        spec_hbm.at[pl.ds(lev * SLOTS, SLOTS)], arrived.at[lev], lsem.at[7]
    )
    for copy in local:
        copy.start()
    own.start()

    def remote(src, dst, ssem, rsem, nb):
        return pltpu.make_async_remote_copy(
            src_ref=src, dst_ref=dst, send_sem=ssem, recv_sem=rsem,
            device_id={"wave": nb}, device_id_type=MESH,
        )

    local[0].wait()
    local[1].wait()

    def repack(l, carry):
        for i in range(ROWS):
            for k in range(5):
                cx[i + 1, l, 8 * k : 8 * k + 8, :] = lon_ref[l, pl.ds(8 * k + i, 8, stride=40), :]
                cy[i + 1, l, 8 * k : 8 * k + 8, :] = lat_ref[l, pl.ds(8 * k + i, 8, stride=40), :]
        return carry


    lax.fori_loop(0, LEVS, repack, 0)

    row = lax.broadcasted_iota(jnp.int32, (640, 1), 0)
    pair_of = 40 * (row % 16) + 8 * (row // 128) + row // 16 % 8
    choose[...] = jnp.where(tbl_ref[...] == pair_of, 1.0, 0.0).astype(BF16)
    lined[...] = jnp.zeros_like(lined)

    pl.semaphore_wait(barrier, 127)

    def spectral_copy(step, s):
        peer = lax.rem(lev + step, LEVS)
        return pltpu.make_async_remote_copy(
            src_ref=spec_hbm.at[peer * SLOTS + s],
            dst_ref=arrived.at[lev, s],
            send_sem=ssend.at[step - 1, s],
            recv_sem=srecv.at[step - 1, s],
            device_id={"lev": peer},
            device_id_type=MESH,
        )

    for s in range(SLOTS):
        for step in range(1, LEVS):
            spectral_copy(step, s).start()
    courant = [
        remote(cx.at[8], cx.at[0], csend.at[0], crecv.at[0], up),
        remote(cy.at[8], cy.at[0], csend.at[1], crecv.at[1], up),
        remote(cx.at[1], cx.at[9], csend.at[2], crecv.at[2], down),
        remote(cy.at[pl.ds(1, 2)], cy.at[pl.ds(9, 2)], csend.at[3], crecv.at[3], down),
    ]
    for copy in courant:
        copy.start()
    for copy in local[2:]:
        copy.wait()
    own.wait()

    klane = lax.broadcasted_iota(jnp.int32, (1, K), 1)

    def legendre_slot(s, carry):
        for step in range(1, LEVS):
            spectral_copy(step, s).wait()
        low = klane < (M - pairs_ref[rank * SLOTS + s])
        spectra = arrived[:, s].reshape(32, K)
        zero = jnp.zeros_like(spectra)
        halves = jnp.concatenate(
            [jnp.where(low, spectra, zero), jnp.where(low, zero, spectra)], 0
        )
        total = dot(halves[:, : K - 1], leg_ref[s, : K - 1, :])
        last = spectra[:, K - 1 : K].astype(F32) * leg_ref[s, K - 1 : K, :].astype(F32)
        total = jnp.concatenate([total[:32], total[32:] + last], 0)
        rounded = total.astype(BF16).astype(F32)
        square = jnp.concatenate([rounded, jnp.zeros_like(rounded)], 0)
        turned[...] = square.T
        for t8 in range(8):
            lined[t8, pl.ds(s, WAVES, stride=8), :] = turned[pl.ds(t8, WAVES, stride=8), :]
        return carry

    for s in range(SLOTS):
        legendre_slot(s, 0)
    total = dot(lined[0].astype(BF16), pack_ref[0])
    for t8 in range(1, 8):
        total += dot(lined[t8].astype(BF16), pack_ref[t8])
    packed = total.astype(BF16)
    for v in range(LEVS):
        msgs[:, v] = packed[:, v * 128 : (v + 1) * 128].reshape(WAVES, 8, 128)

    recv[rank] = msgs[me, lev]

    def scatter(step, carry):
        peer = lax.rem(rank + step, 128)
        pw, pv = peer // LEVS, peer % LEVS
        pltpu.make_async_remote_copy(
            src_ref=msgs.at[pw, pv], dst_ref=recv.at[rank], send_sem=asend, recv_sem=arecv,
            device_id={"wave": pw, "lev": pv}, device_id_type=MESH,
        ).start()
        return carry

    lax.fori_loop(1, 128, scatter, 0)

    for copy in courant:
        copy.wait()
    lanes = lax.broadcasted_iota(jnp.int32, (NF, 128), 1)
    first_lane = lanes == 0
    last_lane = lanes == 127

    def terms(l, carry):
        zero = jnp.zeros((NF, 128), F32)
        cx[0, l] = jnp.where(has_down, cx[0, l], zero)
        cy[0, l] = jnp.where(has_down, cy[0, l], zero)
        cx[9, l] = jnp.where(has_up, cx[9, l], zero)
        cy[9, l] = jnp.where(has_up, cy[9, l], zero)
        cy[10, l] = jnp.where(has_up, cy[10, l], zero)
        for r in range(11):
            v = cy[r, l]
            cyp[r, l] = jnp.maximum(v, 0.0)
            cym[r, l] = jnp.minimum(v, 0.0)
            if r < 10:
                u = cx[r, l]
                cxp[r, l] = jnp.maximum(u, 0.0)
                cxm[r, l] = jnp.minimum(u, 0.0)
        for i in range(ROWS):
            u = cx[i + 1, l]
            ax[i, l] = jnp.abs(u) - u * u
            pair = cy[i + 1, l] + cy[i + 2, l]
            bx[i, l] = (u * 0.125) * (pair + west(pair, first_lane))
        for i in range(ROWS + 1):
            v = cy[i + 1, l]
            ay[i, l] = jnp.abs(v) - v * v
            pair = cx[i + 1, l] + cx[i, l]
            by[i, l] = (v * 0.125) * (pair + east(pair, last_lane))
        return carry


    lax.fori_loop(0, LEVS, terms, 0)

    blocks127 = recv.at[pl.ds(0, 127)]
    pltpu.make_async_copy(blocks127, blocks127, arecv).wait()
    pltpu.make_async_copy(blocks127, blocks127, asend).wait()

    ordered = dot(choose[...], recv[...].reshape(1024, 128))
    for g in range(5):
        qt[g] = ordered[g * 128 : (g + 1) * 128, :].T

    lane = lax.broadcasted_iota(jnp.int32, (8, 128), 1)
    sub = lax.broadcasted_iota(jnp.int32, (8, 128), 0)
    masks = (lane // 16 == sub, lane // 16 == 7 - sub)

    def first(g, carry):
        total = None
        for h in range(2):
            source = g if h == 0 else 4 - g
            rows = slice(h * 128, h * 128 + 128)
            th, tl = hi_ref[g, rows, :], lo_ref[g, rows, :]
            for c in range(2):
                blocks = []
                for x in range(32):
                    line = qt[source, pl.ds(h * 64 + c * 32 + x, 8, stride=0), :]
                    blocks.append(jnp.where(masks[h], line, 0.0))
                lhs = jnp.concatenate(blocks, 0).astype(BF16)
                for table in (th, tl):
                    if c == 1:
                        table = jnp.concatenate([-table[:, 128:], table[:, :128]], 1)
                    term = dot(lhs, table)
                    total = term if total is None else total + term
        total = total.reshape(32, 8, 256)
        at = pl.multiple_of(8 * g, 8)
        ast[:, 0, pl.ds(at, 8), :] = total[:, :, :128]
        ast[:, 1, pl.ds(at, 8), :] = total[:, :, 128:]
        return carry

    lax.fori_loop(0, 5, first, 0)

    def halo_copies(parity, l):
        return [
            remote(stage.at[parity, 1, l], halo.at[parity, 0, l],
                   hsend.at[parity, 0, l], hrecv.at[parity, 0, l], up),
            remote(stage.at[parity, 0, l], halo.at[parity, 1, l],
                   hsend.at[parity, 1, l], hrecv.at[parity, 1, l], down),
        ]

    def send_halo(parity, l):
        for i in range(2):
            stage[parity, 0, l, i] = fld[2 + i, l].astype(BF16)
            stage[parity, 1, l, i] = fld[8 + i, l].astype(BF16)
        for c in halo_copies(parity, l):
            c.start()

    def second(l, carry):
        for t in range(0, ROWS, 2):
            parts = []
            for u in (t, t + 1):
                both = ast[u * 4 + l].reshape(80, 128)
                high = both.astype(BF16)
                low = (both - high.astype(F32)).astype(BF16)
                parts.append(jnp.concatenate([high, high, low], 0))
            values = dot(two_ref[...], jnp.concatenate(parts, 1))
            fld[2 + t, l] = values[:, :128]
            fld[3 + t, l] = values[:, 128:]
        send_halo(0, l)
        return carry

    lax.fori_loop(0, LEVS, second, 0)

    def level_pass(step, carry):
        number = step // LEVS
        l = step % LEVS
        parity = number % 2
        for c in halo_copies(parity, l):
            c.wait()
        zero = jnp.zeros((NF, 128), F32)
        for i in range(2):
            fld[i, l] = jnp.where(has_down, halo[parity, 0, l, i].astype(F32), zero)
            fld[10 + i, l] = jnp.where(has_up, halo[parity, 1, l, i].astype(F32), zero)
        flux = None
        for r in range(-1, 9):
            q = fld[r + 2, l]
            if flux is None:
                flux = cyp[r + 1, l] * fld[r + 1, l] + cym[r + 1, l] * q
            above = cyp[r + 2, l] * q + cym[r + 2, l] * fld[r + 3, l]
            fx = cxp[r + 1, l] * west(q, first_lane) + cxm[r + 1, l] * q
            v = q - (east(fx, last_lane) - fx) - (above - flux)
            flux = above
            if r == -1:
                v = jnp.where(has_down, v, zero)
            if r == 8:
                v = jnp.where(has_up, v, zero)
            w = west(v, first_lane)
            e = east(v, last_lane)
            aw = jnp.abs(w)
            q1s[r + 1] = v
            wst[r + 1] = w
            swe[r + 1] = v + w
            awe[r + 1] = jnp.abs(v) + aw
            dew[r + 1] = e - w
            aew[r + 1] = jnp.abs(e) + aw

        def face(i):
            a, b = q1s[i + 1], q1s[i]
            grad = ratio(a - b, jnp.abs(a) + jnp.abs(b))
            cross = ratio(dew[i + 1] + dew[i], aew[i + 1] + aew[i])
            vy = ay[i, l] * grad - by[i, l] * cross
            gys[i] = jnp.maximum(vy, 0.0) * b + jnp.minimum(vy, 0.0) * a

        def finish(i):
            v, w = q1s[i + 1], wst[i + 1]
            grad = ratio(v - w, awe[i + 1])
            cross = ratio(swe[i + 2] - swe[i], awe[i + 2] + awe[i])
            vx = ax[i, l] * grad - bx[i, l] * cross
            gx = jnp.maximum(vx, 0.0) * w + jnp.minimum(vx, 0.0) * v
            fld[i + 2, l] = v - (east(gx, last_lane) - gx) - (gys[i + 1] - gys[i])

        for i in (0, 1, 2):
            face(i)
        for i in (0, 1):
            finish(i)
        for i in (6, 7, 8):
            face(i)
        for i in (6, 7):
            finish(i)

        @pl.when(number < PASSES - 1)
        def _():
            send_halo(1 - parity, l)

        for i in (3, 4, 5):
            face(i)
        for i in (2, 3, 4, 5):
            finish(i)
        return carry

    lax.fori_loop(0, PASSES * LEVS, level_pass, 0)

    def deliver(l, carry):
        for i in range(ROWS):
            for k in range(5):
                out_ref[l, pl.ds(8 * k + i, 8, stride=40), :] = fld[i + 2, l, 8 * k : 8 * k + 8, :]
        return carry

    lax.fori_loop(0, LEVS, deliver, 0)


def tiles_of(winds):
    return winds.reshape(LEVS, ROWS, NF, NB).transpose(0, 2, 1, 3).reshape(LEVS, NF * ROWS, NB)


def body(spectral, legendre, wave_table, courant_lon, courant_lat):
    table = jnp.pad(wave_table.reshape(128, SLOTS), ((0, 0), (0, 3)), constant_values=-1)
    table = table.reshape(1, 1024)
    parts = spectral.reshape(8, LEVS * SLOTS, K).transpose(1, 0, 2)
    vmem = pl.BlockSpec(memory_space=pltpu.VMEM)
    smem = pl.BlockSpec(memory_space=pltpu.SMEM)
    hbm = pl.BlockSpec(memory_space=pl.ANY)
    high, low = first_stage_tables()
    packing, two = pack_table(), second_stage_table()
    big = lambda rows: pltpu.VMEM((rows, LEVS, NF, NB), F32)
    small = lambda rows: pltpu.VMEM((rows, NF, NB), F32)
    dma = pltpu.SemaphoreType.DMA
    out = pl.pallas_call(
        whole_kernel,
        out_shape=jax.ShapeDtypeStruct((LEVS, NF * ROWS, NB), F32),
        in_specs=[smem, vmem] + [hbm] * 8,
        out_specs=vmem,
        scratch_shapes=[
            pltpu.VMEM(legendre.shape, BF16),
            pltpu.VMEM((LEVS, NF * ROWS, NB), F32),
            pltpu.VMEM((LEVS, NF * ROWS, NB), F32),
            pltpu.VMEM(packing.shape, BF16),
            pltpu.VMEM(high.shape, BF16),
            pltpu.VMEM(low.shape, BF16),
            pltpu.VMEM(two.shape, BF16),
            pltpu.VMEM((LEVS, SLOTS, 8, K), BF16),
            pltpu.VMEM((256, 128), F32),
            pltpu.VMEM((8, 256, 128), F32),
            pltpu.VMEM((WAVES, LEVS, 8, 128), BF16),
            pltpu.VMEM((128, 8, 128), BF16),
            pltpu.VMEM((640, 1024), BF16),
            pltpu.VMEM((5, 128, 128), F32),
            pltpu.VMEM((32, 2, NF, NB), F32),
            big(12), big(10), big(11), big(10), big(10), big(11), big(11),
            big(8), big(8), big(9), big(9),
            small(10), small(10), small(10), small(10), small(10), small(10), small(9),
            pltpu.VMEM((2, 2, LEVS, 2, NF, NB), BF16),
            pltpu.VMEM((2, 2, LEVS, 2, NF, NB), BF16),
            dma((8,)), dma((3, SLOTS)), dma((3, SLOTS)), dma, dma,
            dma((4,)), dma((4,)), dma((2, 2, LEVS)), dma((2, 2, LEVS)),
        ],
        compiler_params=pltpu.CompilerParams(collective_id=0, has_side_effects=True),
        name="whole",
    )(
        wave_table, table, parts, legendre, tiles_of(courant_lon), tiles_of(courant_lat),
        jnp.asarray(packing), jnp.asarray(high), jnp.asarray(low), jnp.asarray(two),
    )
    out = out.reshape(LEVS, NF, ROWS, NB).transpose(0, 2, 1, 3)
    return out.reshape(LEVS, ROWS, NLON)


def solution(mesh):
    placed = (
        P(None, "lev", "wave", None),
        P(("wave", "lev"), None, None),
        P(),
        P("lev", "wave", None),
        P("lev", "wave", None),
    )
    return jax.shard_map(
        body, mesh=mesh, in_specs=placed, out_specs=P("lev", "wave", None), check_vma=False
    )
```

time: 78.4 us -> 62.2 us (0.79)
  waiting for transfers between devices: 18.1 us -> 0 us
  Pallas kernels: 38.8 us -> 56.2 us
  starting transfers between devices: 13.2 us -> 0 us
  local copies, waits for them, and re-layouts: 7.77 us -> 5.67 us
    all_to_all x2 -> x0, waiting for transfers between devices: 18.1 us -> none  [the longest x1 9.92 us: body(): lax.all_to_all(messages.reshape(128, 8, 128), ('wave', 'lev'), split_axis...]
    pallas_call x2 -> x1, Pallas kernels: 38.8 us -> 56.2 us  [body(): pl.pallas_call(whole_kernel, out_shape=jax.ShapeDtypeStruct((LEVS, NF * R...]
    all_to_all x2 -> x0, starting transfers between devices: 13.2 us -> none  [the longest x1 8.67 us: body(): lax.all_to_all(messages.reshape(128, 8, 128), ('wave', 'lev'), split_axis...]
    dynamic_slice x1 -> x0, local copies, waits for them, and re-layouts: 1.3 us -> none  [body(): lax.dynamic_slice_in_dim(wave_table, (wave_rank * LEVS + level_rank) * SL...]
    reshape x2 -> x1, local copies, waits for them, and re-layouts: 2.14 us -> 0.97 us  [body(): parts = spectral.reshape(8, LEVS * SLOTS, K).transpose(1, 0, 2)]
    unnamed x7 -> x2, local copies, waits for them, and re-layouts: 3.44 us -> 3.14 us
  transfers between devices with their start and end apart: 2 -> 0, of which waited for: 2 -> 0; matrix products, arithmetic and copies ran while one was open for 3% -> 0% of each run, Pallas kernels for 0% -> 0%
where the time goes in v2:
time: 62.2 us; the launch traced here: 61.9 us
  Pallas kernels  56.2 us (90%)
  local copies, waits for them, and re-layouts  5.67 us (9%)
    pallas_call x1, Pallas kernels, body(): pl.pallas_call(whole_kernel, out_shape=jax.ShapeDtypeStruct((LEVS, NF * R...  56.2 us
    unnamed x2, local copies, waits for them, and re-layouts  3.14 us

profile of v2, /device:TPU:0, one launch (start us, length us, event | category | flops | bytes accessed | tf_op | source)
XLA Modules:
  0.0 61.9 jit_solution(7965211672562365298)
XLA Ops:
  0.0 0.9 %reshape.27 = s32[128,5]{1,0:T(8,128)S(1)} reshape(s32[640]{0:T(1024)} %pairs_ref.1) | data formatting | bytes 5120 | tf_op jit(solution)/shard_map/reshape | solution.py:406
  0.9 0.7 %reshape.28.tbl_ref = s32[1,1024]{1,0:T(1,128)} reshape(s32[128,8]{1,0:T(8,128)S(1)} %pad.4) | data formatting | bytes 8192 | tf_op jit(solution)/shard_map/reshape | solution.py:407
  1.6 1.2 %copy.11 = bf16[2,4,20,1281]{3,1,0,2:T(4,128)(2,1)S(1)} copy(bf16[2,4,20,1281]{3,1,2,0:T(4,128)(2,1)} %param.9) | data formatting | bytes 819840 | tf_op args[0]
  2.7 1.0 %reshape.29 = bf16[8,20,1281]{2,0,1:T(8,128)(2,1)} reshape(bf16[2,4,20,1281]{3,1,0,2:T(4,128)(2,1)S(1)} %copy.11) | data formatting | bytes 819840 | tf_op jit(solution)/shard_map/reshape | solution.py:408
  3.7 56.2 %whole.1 = f32[4,320,128]{2,1,0:T(8,128)} custom-call(s32[640]{0:T(1024)} %pairs_ref.1, s32[1,1024]{1,0:T(1,128)} %reshape.28.tbl_ref, bf16[20,8,1281]{2,1,0:T(8,128)(2,1)} %bitcast.19, bf16[5,1281,256]{2,1,0:T(8,128)(2,1)} %leg_hbm.1, f32[4,320,128]{2,1,0:T(8,128)} %bitcast.20, f32[4,320,128]{2,1,0:T(8,128)} %bitcast.21, ...), custom_call_target="tpu_custom_call" | custom-call | tf_op jit(solution)/shard_map/whole/pallas_call | solution.py:417
  60.0 2.0 %copy.13 = f32[4,8,5120]{2,1,0:T(8,128)} copy(f32[4,8,5120]{2,1,0:T(8,128)} %bitcast.18) | data formatting | bytes 1310720
  (1 shorter events, 0.0 us)

commit v3 on v2

v3 whole, which is shorter than its diff:
```python
import math

import jax
import jax.numpy as jnp
import numpy as np
from jax import lax
from jax.experimental import pallas as pl
from jax.experimental.pallas import tpu as pltpu
from jax.sharding import PartitionSpec as P

M = 1280
NLON = 5120
K = 1281
PASSES = 4
WAVES = 32
LEVS = 4
SLOTS = 5
ROWS = 8
NF = 40
NB = 128
F32 = jnp.float32
BF16 = jnp.bfloat16
MESH = pl.DeviceIdType.MESH


def split_table(values):
    high = values.astype(np.float32).astype(BF16)
    low = (values - high.astype(np.float64)).astype(np.float32).astype(BF16)
    return high, low


def first_stage_tables():
    g = np.arange(5)[:, None, None, None]
    h = np.arange(2)[None, :, None, None]
    f8 = np.arange(8)[None, None, :, None]
    p1 = np.arange(16)[None, None, None, :]
    m = np.where(h == 0, 40 * p1 + 8 * g + f8, M - 1 - (40 * p1 + 8 * (4 - g) + f8))
    m = m.reshape(5, 256, 1)
    angle = 2.0 * math.pi / NLON * ((m * np.arange(NB)[None, None, :]) % NLON)
    weight = np.where(m == 0, 1.0, 2.0)
    return split_table(np.concatenate([weight * np.cos(angle), weight * np.sin(angle)], -1))


def second_stage_table():
    row = np.arange(NF)
    place = 5 * (row % 8) + row // 8
    angle = 2.0 * math.pi / NF * ((place[:, None] * np.arange(NF)[None, :]) % NF)
    high, low = split_table(np.concatenate([np.cos(angle), -np.sin(angle)], -1))
    return np.concatenate([high, low, high], -1)


def pack_table():
    t8 = np.arange(8)[:, None, None]
    lane = np.arange(128)[None, :, None]
    h, v, c, l = lane // 32, lane // 8 % 4, lane // 4 % 2, lane % 4
    goal = v * 128 + h * 64 + c * 32 + t8 * 4 + l
    hit = (goal == np.arange(512)[None, None, :]) & (lane < 64)
    return hit.astype(np.float32).astype(BF16)


def dot(a, b):
    return jnp.dot(a, b, preferred_element_type=F32)


def west(v, edge):
    r = pltpu.roll(v, 1, 1)
    before = jnp.concatenate([pltpu.roll(r[32:40], 1, 0), r[0:32]], 0)
    return jnp.where(edge, before, r)


def east(v, edge):
    r = pltpu.roll(v, 127, 1)
    after = jnp.concatenate([r[8:40], pltpu.roll(r[0:8], 7, 0)], 0)
    return jnp.where(edge, after, r)


def ratio(x, y):
    return x / jnp.maximum(y, 1.0)


def donor(u, low, high):
    return u * jnp.where(u > 0.0, low, high)


def whole_kernel(
    pairs_ref, spec_hbm, leg_hbm, lon_hbm, lat_hbm, pack_hbm, hi_hbm, lo_hbm, two_hbm,
    out_ref,
    spec_ref, leg_ref, lon_ref, lat_ref, pack_ref, hi_ref, lo_ref, two_ref,
    padded, sorted_ref, arrived, turned, lined, msgs, recv, column, choose,
    qt, ast, fld, cx, cy, cxp, cxm, cyp, cym, ax, bx, ay, by,
    q1s, abv, wst, swe, awe, dew, aew, gys, stage, halo, cstage, chalo,
    lsem, ssend, srecv, asend, arecv, csend, crecv, hsend, hrecv, round_sem,
):
    me = lax.axis_index("wave")
    lev = lax.axis_index("lev")
    rank = me * LEVS + lev
    up = lax.rem(me + 1, WAVES)
    down = lax.rem(me + WAVES - 1, WAVES)
    has_up = me < WAVES - 1
    has_down = me > 0

    at_z, at_x, at_y = me // 8, me // 4 % 2, me % 4
    z_peers = [lax.rem(me + 8 * n, WAVES) for n in (1, 2, 3)]
    y_peers = [me - at_y + lax.rem(at_y + n, 4) for n in (1, 2, 3)]
    x_peer = me + 4 - 8 * at_x
    barrier = pltpu.get_barrier_semaphore()

    def signal(sem, where):
        pl.semaphore_signal(sem, inc=1, device_id=where, device_id_type=MESH)

    for n in (1, 2, 3):
        signal(barrier, {"lev": lax.rem(lev + n, LEVS)})
    for peer in y_peers + z_peers + [x_peer]:
        signal(barrier, {"wave": peer})

    local = [
        pltpu.make_async_copy(a, b, lsem.at[n])
        for n, (a, b) in enumerate(
            [(spec_hbm, spec_ref), (lon_hbm, lon_ref), (lat_hbm, lat_ref), (leg_hbm, leg_ref),
             (pack_hbm, pack_ref), (hi_hbm, hi_ref), (lo_hbm, lo_ref), (two_hbm, two_ref)]
        )
    ]
    for copy in local:
        copy.start()

    def remote(src, dst, ssem, rsem, nb):
        return pltpu.make_async_remote_copy(
            src_ref=src, dst_ref=dst, send_sem=ssem, recv_sem=rsem,
            device_id={"wave": nb}, device_id_type=MESH,
        )

    goal = lax.broadcasted_iota(jnp.int32, (160, 256), 0)
    origin = lax.broadcasted_iota(jnp.int32, (160, 256), 1)
    moves = (goal // 8 == origin % 32) & (goal % 8 == origin // 32)
    padded[:, 16:32, :] = jnp.zeros((8, 16, K), BF16)
    local[0].wait()
    for n in range(8):
        padded[n, 0:20, :] = spec_ref[n]
    by_slot = dot(jnp.where(moves, 1.0, 0.0).astype(BF16), padded[...].reshape(256, K))
    sorted_ref[...] = by_slot.astype(BF16).reshape(20, 8, K)

    pl.semaphore_wait(barrier, 10)

    def spectral_copy(step, s):
        peer = lax.rem(lev + step, LEVS)
        return pltpu.make_async_remote_copy(
            src_ref=sorted_ref.at[peer * SLOTS + s],
            dst_ref=arrived.at[lev, s],
            send_sem=ssend.at[step - 1, s],
            recv_sem=srecv.at[step - 1, s],
            device_id={"lev": peer},
            device_id_type=MESH,
        )

    for s in range(SLOTS):
        for step in range(1, LEVS):
            spectral_copy(step, s).start()
    for peer in y_peers + z_peers:
        signal(round_sem.at[0], {"wave": peer})
    for s in range(SLOTS):
        arrived[lev, s] = sorted_ref[lev * SLOTS + s]

    local[1].wait()
    local[2].wait()

    def repack(l, carry):
        for i in range(ROWS):
            for k in range(5):
                cx[i + 1, l, 8 * k : 8 * k + 8, :] = lon_ref[l, pl.ds(8 * k + i, 8, stride=40), :]
                cy[i + 1, l, 8 * k : 8 * k + 8, :] = lat_ref[l, pl.ds(8 * k + i, 8, stride=40), :]
        cstage[0, l] = cx[8, l].astype(BF16)
        cstage[1, l] = cy[8, l].astype(BF16)
        cstage[2, l] = cx[1, l].astype(BF16)
        cstage[3, l] = cy[1, l].astype(BF16)
        cstage[4, l] = cy[2, l].astype(BF16)
        return carry

    lax.fori_loop(0, LEVS, repack, 0)

    pl.semaphore_wait(round_sem.at[0], 6)
    for n in (1, 2, 3):
        signal(round_sem.at[1], {"wave": lax.rem(me + 8 * n, WAVES)})
    for n in (0, 1, 2, 3):
        signal(round_sem.at[1], {"wave": lax.rem(x_peer + 8 * n, WAVES)})

    column[...] = jnp.full((1024, 128), -1, jnp.int32)

    def spread(n, carry):
        for s in range(SLOTS):
            column[pl.ds(n * 8 + s, 1), :] = jnp.full((1, 128), pairs_ref[n * SLOTS + s], jnp.int32)
        return carry

    lax.fori_loop(0, 128, spread, 0)
    place = lax.broadcasted_iota(jnp.int32, (1, 128), 1)
    for g in range(5):
        pair_of = 40 * (place % 16) + 8 * g + place // 16
        choose[:, g * 128 : (g + 1) * 128] = jnp.where(
            column[...] == pair_of, 1.0, 0.0
        ).astype(BF16)
    lined[...] = jnp.zeros_like(lined)

    lanes = lax.broadcasted_iota(jnp.int32, (NF, 128), 1)
    first_lane = lanes == 0
    last_lane = lanes == 127

    def split_x(r, l):
        u = cx[r, l]
        cxp[r, l] = jnp.maximum(u, 0.0)
        cxm[r, l] = jnp.minimum(u, 0.0)

    def split_y(r, l):
        v = cy[r, l]
        cyp[r, l] = jnp.maximum(v, 0.0)
        cym[r, l] = jnp.minimum(v, 0.0)

    def cross_x(i, l):
        pair = cy[i + 1, l] + cy[i + 2, l]
        bx[i, l] = (cx[i + 1, l] * 0.125) * (pair + west(pair, first_lane))

    def cross_y(i, l):
        pair = cx[i + 1, l] + cx[i, l]
        by[i, l] = (cy[i + 1, l] * 0.125) * (pair + east(pair, last_lane))

    def terms(l, carry):
        for i in range(ROWS):
            split_x(i + 1, l)
            split_y(i + 1, l)
            u = cx[i + 1, l]
            ax[i, l] = jnp.abs(u) - u * u
            v = cy[i + 1, l]
            ay[i, l] = jnp.abs(v) - v * v
            if i < ROWS - 1:
                cross_x(i, l)
            if i > 0:
                cross_y(i, l)
        return carry

    lax.fori_loop(0, LEVS, terms, 0)
    for copy in local[3:]:
        copy.wait()

    klane = lax.broadcasted_iota(jnp.int32, (1, K), 1)
    for s in range(SLOTS):
        for step in range(1, LEVS):
            spectral_copy(step, s).wait()
        low = klane < (M - pairs_ref[rank * SLOTS + s])
        spectra = arrived[:, s].reshape(32, K)
        zero = jnp.zeros_like(spectra)
        halves = jnp.concatenate(
            [jnp.where(low, spectra, zero), jnp.where(low, zero, spectra)], 0
        )
        total = dot(halves[:, : K - 1], leg_ref[s, : K - 1, :])
        last = spectra[:, K - 1 : K].astype(F32) * leg_ref[s, K - 1 : K, :].astype(F32)
        total = jnp.concatenate([total[:32], total[32:] + last], 0)
        rounded = total.astype(BF16).astype(F32)
        square = jnp.concatenate([rounded, jnp.zeros_like(rounded)], 0)
        turned[...] = square.T
        for t8 in range(8):
            lined[t8, pl.ds(s, WAVES, stride=8), :] = turned[pl.ds(t8, WAVES, stride=8), :]
    total = dot(lined[0].astype(BF16), pack_ref[0])
    for t8 in range(1, 8):
        total += dot(lined[t8].astype(BF16), pack_ref[t8])
    packed = total.astype(BF16)
    for v in range(LEVS):
        msgs[:, v] = packed[:, v * 128 : (v + 1) * 128].reshape(WAVES, 8, 128)

    pl.semaphore_wait(round_sem.at[1], 7)

    def scatter(step, carry):
        peer = lax.rem(rank + step, 128)
        pw, pv = peer // LEVS, peer % LEVS
        pltpu.make_async_remote_copy(
            src_ref=msgs.at[pw, pv], dst_ref=recv.at[rank], send_sem=asend, recv_sem=arecv,
            device_id={"wave": pw, "lev": pv}, device_id_type=MESH,
        ).start()
        return carry

    lax.fori_loop(1, 128, scatter, 0)
    recv[rank] = msgs[me, lev]
    courant = [
        remote(cstage.at[pl.ds(0, 2)], chalo.at[pl.ds(0, 2)], csend.at[0], crecv.at[0], up),
        remote(cstage.at[pl.ds(2, 3)], chalo.at[pl.ds(2, 3)], csend.at[1], crecv.at[1], down),
    ]
    for copy in courant:
        copy.start()

    blocks127 = recv.at[pl.ds(0, 127)]
    pltpu.make_async_copy(blocks127, blocks127, arecv).wait()
    pltpu.make_async_copy(blocks127, blocks127, asend).wait()

    ordered = lax.dot_general(
        recv[...].reshape(1024, 128), choose[...], (((0,), (0,)), ((), ())),
        preferred_element_type=F32,
    )
    for g in range(5):
        qt[g] = ordered[:, g * 128 : (g + 1) * 128]

    lane = lax.broadcasted_iota(jnp.int32, (8, 128), 1)
    sub = lax.broadcasted_iota(jnp.int32, (8, 128), 0)
    masks = (lane // 16 == sub, lane // 16 == 7 - sub)

    def first(g, carry):
        total = None
        for h in range(2):
            source = g if h == 0 else 4 - g
            rows = slice(h * 128, h * 128 + 128)
            th, tl = hi_ref[g, rows, :], lo_ref[g, rows, :]
            for c in range(2):
                blocks = []
                for x in range(32):
                    line = qt[source, pl.ds(h * 64 + c * 32 + x, 8, stride=0), :]
                    blocks.append(jnp.where(masks[h], line, 0.0))
                lhs = jnp.concatenate(blocks, 0).astype(BF16)
                for table in (th, tl):
                    if c == 1:
                        table = jnp.concatenate([-table[:, 128:], table[:, :128]], 1)
                    term = dot(lhs, table)
                    total = term if total is None else total + term
        total = total.reshape(32, 8, 256)
        at = pl.multiple_of(8 * g, 8)
        ast[:, 0, pl.ds(at, 8), :] = total[:, :, :128]
        ast[:, 1, pl.ds(at, 8), :] = total[:, :, 128:]
        return carry

    lax.fori_loop(0, 5, first, 0)

    def halo_copies(parity, l):
        return [
            remote(stage.at[parity, 1, l], halo.at[parity, 0, l],
                   hsend.at[parity, 0, l], hrecv.at[parity, 0, l], up),
            remote(stage.at[parity, 0, l], halo.at[parity, 1, l],
                   hsend.at[parity, 1, l], hrecv.at[parity, 1, l], down),
        ]

    def send_halo(parity, l):
        for i in range(2):
            stage[parity, 0, l, i] = fld[2 + i, l].astype(BF16)
            stage[parity, 1, l, i] = fld[8 + i, l].astype(BF16)
        for c in halo_copies(parity, l):
            c.start()

    def second(l, carry):
        for t in range(0, ROWS, 2):
            parts = []
            for u in (t, t + 1):
                both = ast[u * 4 + l].reshape(80, 128)
                high = both.astype(BF16)
                low = (both - high.astype(F32)).astype(BF16)
                parts.append(jnp.concatenate([high, high, low], 0))
            values = dot(two_ref[...], jnp.concatenate(parts, 1))
            fld[2 + t, l] = values[:, :128]
            fld[3 + t, l] = values[:, 128:]
        send_halo(0, l)
        return carry

    lax.fori_loop(0, LEVS, second, 0)

    zero = jnp.zeros((NF, 128), F32)

    def upwind(rows, l):
        flux = None
        for r in rows:
            q = fld[r + 2, l]
            if flux is None:
                flux = cyp[r + 1, l] * fld[r + 1, l] + cym[r + 1, l] * q
            above = cyp[r + 2, l] * q + cym[r + 2, l] * fld[r + 3, l]
            fx = cxp[r + 1, l] * west(q, first_lane) + cxm[r + 1, l] * q
            v = q - (east(fx, last_lane) - fx) - (above - flux)
            flux = above
            if r == -1:
                v = jnp.where(has_down, v, zero)
            if r == 8:
                v = jnp.where(has_up, v, zero)
            w = west(v, first_lane)
            e = east(v, last_lane)
            av = jnp.abs(v)
            aw = jnp.abs(w)
            q1s[l, r + 1] = v
            abv[l, r + 1] = av
            wst[l, r + 1] = w
            swe[l, r + 1] = v + w
            awe[l, r + 1] = av + aw
            dew[l, r + 1] = e - w
            aew[l, r + 1] = jnp.abs(e) + aw

    def face(i, l):
        a, b = q1s[l, i + 1], q1s[l, i]
        grad = ratio(a - b, abv[l, i + 1] + abv[l, i])
        cross = ratio(dew[l, i + 1] + dew[l, i], aew[l, i + 1] + aew[l, i])
        gys[l, i] = donor(ay[i, l] * grad - by[i, l] * cross, b, a)

    def finish(i, l):
        v, w = q1s[l, i + 1], wst[l, i + 1]
        grad = ratio(v - w, awe[l, i + 1])
        cross = ratio(swe[l, i + 2] - swe[l, i], awe[l, i + 2] + awe[l, i])
        gx = donor(ax[i, l] * grad - bx[i, l] * cross, w, v)
        fld[i + 2, l] = v - (east(gx, last_lane) - gx) - (gys[l, i + 1] - gys[l, i])

    def inner(l):
        upwind((1, 2, 3, 4, 5, 6), l)
        for i in (2, 3, 4, 5, 6):
            face(i, l)
        for i in (2, 3, 4, 5):
            finish(i, l)

    def outer(parity, l):
        for c in halo_copies(parity, l):
            c.wait()
        for i in range(2):
            fld[i, l] = jnp.where(has_down, halo[parity, 0, l, i].astype(F32), zero)
            fld[10 + i, l] = jnp.where(has_up, halo[parity, 1, l, i].astype(F32), zero)
        upwind((-1, 0), l)
        upwind((7, 8), l)
        for i in (0, 1, 7, 8):
            face(i, l)
        for i in (0, 1, 6, 7):
            finish(i, l)

    def first_inner(l, carry):
        inner(l)
        return carry

    lax.fori_loop(0, LEVS, first_inner, 0)
    for copy in courant:
        copy.wait()

    def first_outer(l, carry):
        cx[0, l] = jnp.where(has_down, chalo[0, l].astype(F32), zero)
        cy[0, l] = jnp.where(has_down, chalo[1, l].astype(F32), zero)
        cx[9, l] = jnp.where(has_up, chalo[2, l].astype(F32), zero)
        cy[9, l] = jnp.where(has_up, chalo[3, l].astype(F32), zero)
        cy[10, l] = jnp.where(has_up, chalo[4, l].astype(F32), zero)
        for r in (0, 9):
            split_x(r, l)
        for r in (0, 9, 10):
            split_y(r, l)
        v = cy[9, l]
        ay[8, l] = jnp.abs(v) - v * v
        cross_x(7, l)
        cross_y(0, l)
        cross_y(8, l)
        outer(0, l)
        send_halo(1, l)
        return carry

    lax.fori_loop(0, LEVS, first_outer, 0)

    def level_pass(step, carry):
        number = step // LEVS
        l = step % LEVS
        parity = number % 2
        inner(l)
        outer(parity, l)

        @pl.when(number < PASSES - 1)
        def _():
            send_halo(1 - parity, l)

        return carry

    lax.fori_loop(LEVS, PASSES * LEVS, level_pass, 0)

    def deliver(l, carry):
        for i in range(ROWS):
            for k in range(5):
                out_ref[l, pl.ds(8 * k + i, 8, stride=40), :] = fld[i + 2, l, 8 * k : 8 * k + 8, :]
        return carry

    lax.fori_loop(0, LEVS, deliver, 0)


def tiles_of(winds):
    return winds.reshape(LEVS, ROWS, NF, NB).transpose(0, 2, 1, 3).reshape(LEVS, NF * ROWS, NB)


def body(spectral, legendre, wave_table, courant_lon, courant_lat):
    parts = spectral.reshape(8, LEVS * SLOTS, K)
    vmem = pl.BlockSpec(memory_space=pltpu.VMEM)
    smem = pl.BlockSpec(memory_space=pltpu.SMEM)
    hbm = pl.BlockSpec(memory_space=pl.ANY)
    high, low = first_stage_tables()
    packing, two = pack_table(), second_stage_table()
    big = lambda rows: pltpu.VMEM((rows, LEVS, NF, NB), F32)
    small = lambda rows: pltpu.VMEM((LEVS, rows, NF, NB), F32)
    dma = pltpu.SemaphoreType.DMA
    out = pl.pallas_call(
        whole_kernel,
        out_shape=jax.ShapeDtypeStruct((LEVS, NF * ROWS, NB), F32),
        in_specs=[smem] + [hbm] * 8,
        out_specs=vmem,
        scratch_shapes=[
            pltpu.VMEM((8, LEVS * SLOTS, K), BF16),
            pltpu.VMEM(legendre.shape, BF16),
            pltpu.VMEM((LEVS, NF * ROWS, NB), F32),
            pltpu.VMEM((LEVS, NF * ROWS, NB), F32),
            pltpu.VMEM(packing.shape, BF16),
            pltpu.VMEM(high.shape, BF16),
            pltpu.VMEM(low.shape, BF16),
            pltpu.VMEM(two.shape, BF16),
            pltpu.VMEM((8, 32, K), BF16),
            pltpu.VMEM((LEVS * SLOTS, 8, K), BF16),
            pltpu.VMEM((LEVS, SLOTS, 8, K), BF16),
            pltpu.VMEM((256, 128), F32),
            pltpu.VMEM((8, 256, 128), F32),
            pltpu.VMEM((WAVES, LEVS, 8, 128), BF16),
            pltpu.VMEM((128, 8, 128), BF16),
            pltpu.VMEM((1024, 128), jnp.int32),
            pltpu.VMEM((1024, 640), BF16),
            pltpu.VMEM((5, 128, 128), F32),
            pltpu.VMEM((32, 2, NF, NB), F32),
            big(12), big(10), big(11), big(10), big(10), big(11), big(11),
            big(8), big(8), big(9), big(9),
            *[small(10)] * 7, small(9),
            pltpu.VMEM((2, 2, LEVS, 2, NF, NB), BF16),
            pltpu.VMEM((2, 2, LEVS, 2, NF, NB), BF16),
            pltpu.VMEM((5, LEVS, NF, NB), BF16),
            pltpu.VMEM((5, LEVS, NF, NB), BF16),
            dma((8,)), dma((3, SLOTS)), dma((3, SLOTS)), dma, dma,
            dma((2,)), dma((2,)), dma((2, 2, LEVS)), dma((2, 2, LEVS)),
            pltpu.SemaphoreType.REGULAR((2,)),
        ],
        compiler_params=pltpu.CompilerParams(collective_id=0, has_side_effects=True),
        name="whole",
    )(
        wave_table, parts, legendre, tiles_of(courant_lon), tiles_of(courant_lat),
        jnp.asarray(packing), jnp.asarray(high), jnp.asarray(low), jnp.asarray(two),
    )
    out = out.reshape(LEVS, NF, ROWS, NB).transpose(0, 2, 1, 3)
    return out.reshape(LEVS, ROWS, NLON)


def solution(mesh):
    placed = (
        P(None, "lev", "wave", None),
        P(("wave", "lev"), None, None),
        P(),
        P("lev", "wave", None),
        P("lev", "wave", None),
    )
    return jax.shard_map(
        body, mesh=mesh, in_specs=placed, out_specs=P("lev", "wave", None), check_vma=False
    )
```

time: 62.2 us -> 56.6 us (0.910)
  Pallas kernels: 56.2 us -> 52.6 us
  local copies, waits for them, and re-layouts: 5.67 us -> 3.84 us
    pallas_call x1, Pallas kernels: 56.2 us -> 52.6 us  [body(): pl.pallas_call(whole_kernel, out_shape=jax.ShapeDtypeStruct((LEVS, NF * R...]
    reshape x3 -> x0, local copies, waits for them, and re-layouts: 2.52 us -> none  [the longest x1 0.97 us: body(): parts = spectral.reshape(8, LEVS * SLOTS, K).transpose(1, 0, 2)]
    unnamed x2, local copies, waits for them, and re-layouts: 3.14 us -> 3.84 us
where the time goes in v3:
time: 56.6 us; the launch traced here: 56.4 us
  Pallas kernels  52.6 us (93%)
  local copies, waits for them, and re-layouts  3.84 us (7%)
    pallas_call x1, Pallas kernels, body(): pl.pallas_call(whole_kernel, out_shape=jax.ShapeDtypeStruct((LEVS, NF * R...  52.6 us
    unnamed x2, local copies, waits for them, and re-layouts  3.84 us

profile of v3, /device:TPU:0, one launch (start us, length us, event | category | flops | bytes accessed | tf_op | source)
XLA Modules:
  0.0 56.4 jit_solution(16840716282462738634)
XLA Ops:
  0.0 1.9 %copy.10 = bf16[2,4,20,1281]{3,2,1,0:T(8,128)(2,1)} copy(bf16[2,4,20,1281]{3,1,2,0:T(4,128)(2,1)} %param.9) | data formatting | bytes 819840 | tf_op args[0]
  1.9 52.6 %whole.1 = f32[4,320,128]{2,1,0:T(8,128)} custom-call(s32[640]{0:T(1024)} %pairs_ref.1, bf16[8,20,1281]{2,1,0:T(8,128)(2,1)} %bitcast.17, bf16[5,1281,256]{2,1,0:T(8,128)(2,1)} %leg_hbm.1, f32[4,320,128]{2,1,0:T(8,128)} %bitcast.18, f32[4,320,128]{2,1,0:T(8,128)} %bitcast.19, bf16[8,128,512]{2,1,0:T(8,128)(2,1)} %constant.8.clone.pack_hbm, ...), custom_call_target="tpu_custom_call" | custom-call | tf_op jit(solution)/shard_map/whole/pallas_call | solution.py:486
  54.4 2.0 %copy.12 = f32[4,8,5120]{2,1,0:T(8,128)} copy(f32[4,8,5120]{2,1,0:T(8,128)} %bitcast.16) | data formatting | bytes 1310720
